TPU v7x, 256 devices: a whole 4x4x8 slice. The times are simulated.
256 devices in a mesh: ctx: 64 (over x, z, core), cache: 4 (over y).
Axes of the slice: x: 4, y: 4, z: 8, core: 2. Of those that a mesh axis runs over, the one named last changes fastest.
Arguments:
- queries: bfloat16 [8192, 8192], P('ctx'), may hold values from -6 to 6
- keys: bfloat16 [192, 64, 8192], P('cache', None, 'ctx'), may hold values from -6 to 6
- values: bfloat16 [192, 64, 8192], P('cache', None, 'ctx'), may hold values from -6 to 6
- block_imgs: int32 [32, 16], replicated, may hold values from 0 to 192, as said below
- img_req: int32 [192], replicated, may hold values from 0 to 31, as said below
- req_start: int32 [32], replicated, may hold values from 0 to 8064, as said below
Outputs:
- attended: bfloat16 [8192, 8192], P('ctx')
Inputs may be any that keep to these rules, and one draw needn't show every extreme that they name: `block_imgs`: row b holds in slots 0 to 7 the images of request b - 1 (empty for b = 0) and in slots 8 to 15 those of request b; a request without images leaves its slots empty; the value 192 marks an empty slot; some rows are full. `img_req`: every request with images owns exactly 8 of them; 8 requests own none; the first and the last request own images. req_start[0] = 0, and request r begins inside text block r after the block's first token, at most 128 tokens in, so block b holds the tail of request b - 1 and the head of request b.
All inputs are finite; a program needn't handle non-finite values.
Results may differ from a plain program's by a relative error of at most 0.005.
Values may be sent and summed in bfloat16 or wider, within the bound.
A program may use at most 128 MiB of HBM per device.

v0:
```python
import jax
import jax.numpy as jnp
from jax import lax
from jax.sharding import PartitionSpec as P

HD = 128


MASKED_SCORE = -1e30


def merged(part, axis, combine):
    gathered = jax.tree.map(lambda a: lax.all_gather(a, axis), part)

    def take(source):
        return jax.tree.map(lambda a: lax.dynamic_index_in_dim(a, source, 0, False), gathered)

    return lax.fori_loop(
        1, lax.axis_size(axis), lambda source, state: combine(state, take(source)), take(0)
    )


def attend(
    query_rows,
    img_lists,
    key_cache,
    value_cache,
    img_req,
    req_start,
    first_img,
    tok_starts,
    block_len,
):
    group_count = img_lists.shape[0]
    slot_count = img_lists.shape[1]
    held_count = key_cache.shape[0]
    latent_count = key_cache.shape[1]
    head_count = key_cache.shape[2] // HD
    image_count = img_req.shape[0]
    local_index = img_lists - first_img
    present = (img_lists < image_count) & (local_index >= 0) & (local_index < held_count)
    safe_local = jnp.clip(local_index, 0, held_count - 1)
    key_rows = key_cache[safe_local].reshape(group_count, slot_count * latent_count, head_count, HD)
    value_rows = value_cache[safe_local].reshape(
        group_count, slot_count * latent_count, head_count, HD
    )
    owners = img_req[jnp.clip(img_lists, 0, image_count - 1)]
    position = tok_starts[:, None] + jnp.arange(block_len, dtype=jnp.int32)[None, :]
    req_tok = (
        jnp.sum((req_start[None, None, :] <= position[:, :, None]).astype(jnp.int32), axis=2) - 1
    )
    visible = present[:, None, :] & (owners[:, None, :] == req_tok[:, :, None])
    key_mask = jnp.repeat(visible, latent_count, axis=2)[:, None]
    query_blocks = query_rows.reshape(group_count, block_len, head_count, HD)
    scores = jnp.einsum(
        "gthd,gkhd->ghtk", query_blocks, key_rows, preferred_element_type=jnp.float32
    ) * HD ** (-0.5)
    top_score = jnp.max(jnp.where(key_mask, scores, MASKED_SCORE), axis=-1)
    weights = jnp.where(key_mask, jnp.exp(scores - top_score[..., None]), 0.0)
    total_weight = jnp.sum(weights, axis=-1)
    numerator = jnp.einsum(
        "ghtk,gkhd->gthd",
        weights.astype(jnp.bfloat16),
        value_rows,
        preferred_element_type=jnp.float32,
    )
    return (top_score, total_weight, numerator)


def combine(first_state, second_state):
    top_left, total_left, numer_left = first_state
    top_right, total_right, numer_right = second_state
    top_both = jnp.maximum(top_left, top_right)
    left_scale = jnp.exp(top_left - top_both)
    right_scale = jnp.exp(top_right - top_both)
    total_both = total_left * left_scale + total_right * right_scale
    numer_both = (
        numer_left * jnp.transpose(left_scale)[:, :, None]
        + numer_right * jnp.transpose(right_scale)[:, :, None]
    )
    return (top_both, total_both, numer_both)


def shards(queries, keys, values, block_imgs, img_req, req_start):
    head_rows = lax.all_to_all(queries, "ctx", split_axis=1, concat_axis=0, tiled=True)
    tokens = head_rows.shape[0]
    block_count = block_imgs.shape[0]
    block_len = tokens // block_count
    feature_width = head_rows.shape[1]
    head_count = feature_width // HD
    first_img = lax.axis_index("cache") * keys.shape[0]
    group_size = 2
    step_count = block_count // group_size

    def one_step(step_index):
        row_slice = lax.dynamic_slice_in_dim(
            head_rows, step_index * group_size * block_len, group_size * block_len, 0
        )
        img_lists = lax.dynamic_slice_in_dim(block_imgs, step_index * group_size, group_size, 0)
        starts = (
            step_index * group_size * block_len
            + jnp.arange(group_size, dtype=jnp.int32) * block_len
        )
        return attend(
            row_slice, img_lists, keys, values, img_req, req_start, first_img, starts, block_len
        )

    top_score, total_weight, numerator = lax.map(one_step, jnp.arange(step_count, dtype=jnp.int32))
    top_score = jnp.transpose(top_score, (2, 0, 1, 3)).reshape(head_count, tokens)
    total_weight = jnp.transpose(total_weight, (2, 0, 1, 3)).reshape(head_count, tokens)
    numerator = numerator.reshape(tokens, head_count, HD)
    top_score, total_weight, numerator = merged(
        (top_score, total_weight, numerator), "cache", combine
    )
    denom = jnp.where(total_weight > 0, total_weight, 1.0)
    head_output = (
        (numerator / jnp.transpose(denom)[:, :, None])
        .astype(jnp.bfloat16)
        .reshape(tokens, feature_width)
    )
    token_output = lax.all_to_all(head_output, "ctx", split_axis=0, concat_axis=1, tiled=True)
    return token_output


def solution(mesh):
    placed = (P("ctx", None), P("cache", None, "ctx"), P("cache", None, "ctx"), P(), P(), P())
    return jax.shard_map(
        shards, mesh=mesh, in_specs=placed, out_specs=P("ctx", None), check_vma=False
    )
```

profile of v0, /device:TPU:16, one launch (start us, length us, event | category | flops | bytes accessed | tf_op | source)
XLA Modules:
  0.0 683.2 jit_solution(11241406196247934807)
XLA Ops:
  8.1 1.9 copy_bitcast_fusion
  10.0 12.3 %all-to-all-start = ((bf16[128,64,128]{2,0,1:T(8,128)(2,1)}), bf16[128,64,128]{2,0,1:T(8,128)(2,1)}, u32[]{:S(2)}, u32[]{:S(2)}) async-start(bf16[128,64,128]{2,0,1:T(8,128)(2,1)} %copy_bitcast_fusion), calls=%async_computation | async-start | bytes 4194304 | tf_op jit(solution)/shard_map/all_to_all | solution.py:85
  23.1 50.2 %all-to-all-done = bf16[128,64,128]{2,0,1:T(8,128)(2,1)} async-done(((bf16[128,64,128]{2,0,1:T(8,128)(2,1)}), bf16[128,64,128]{2,0,1:T(8,128)(2,1)}, u32[]{:S(2)}, u32[]{:S(2)}) %all-to-all-start) | async-done | bytes 2097184 | tf_op jit(solution)/shard_map/all_to_all | solution.py:85
  73.4 251.9 %while.35 = (s32[]{:T(128)}, f32[16,2,1,256]{3,1,2,0:T(2,128)}, f32[16,2,1,256]{3,2,1,0:T(1,128)}, f32[16,2,256,1,128]{4,2,1,0,3:T(8,128)}, s32[16]{0:T(128)S(1)...) while((s32[]{:T(128)}, f32[16,2,1,256]{3,1,2,0:T(2,128)}, ...), condition=%wide.region_4.5_spmd, body=%wide.region_0.4_spmd.sunk | while | flops 274270208 | bytes 14342921 | solution.py:108
  79.6 1.8 gather_fusion.2
  81.4 2.5 gather_fusion.1
  95.4 1.8 gather_fusion.2
  97.2 2.5 gather_fusion.1
  111.1 1.8 gather_fusion.2
  112.9 2.5 gather_fusion.1
  126.9 1.8 gather_fusion.2
  128.7 2.5 gather_fusion.1
  142.6 1.8 gather_fusion.2
  144.4 2.5 gather_fusion.1
  158.3 1.8 gather_fusion.2
  160.1 2.5 gather_fusion.1
  174.1 1.8 gather_fusion.2
  175.9 2.5 gather_fusion.1
  189.8 1.8 gather_fusion.2
  191.6 2.5 gather_fusion.1
  205.5 1.8 gather_fusion.2
  207.3 2.5 gather_fusion.1
  221.3 1.8 gather_fusion.2
  223.1 2.5 gather_fusion.1
  238.8 2.5 gather_fusion.1
  254.6 2.5 gather_fusion.1
  270.3 2.5 gather_fusion.1
  286.1 2.5 gather_fusion.1
  301.8 2.5 gather_fusion.1
  317.5 2.5 gather_fusion.1
  326.1 10.8 %all_gather.9 = f32[4,1,8192]{2,1,0:T(1,128)S(1)} all-gather(f32[1,1,8192]{2,1,0:T(1,128)S(1)} %all_gather_reshape_transpose.6), channel_id=1, replica_groups=mesh['ctx'=64,'cache'=4] {'cache'}, dimensions={0}, use_global_device_ids=true | all-gather | bytes 163840 | tf_op jit(solution)/shard_map/all_gather | solution.py:13
  336.9 12.7 %all_gather.10 = f32[4,1,8192]{2,1,0:T(1,128)S(1)} all-gather(f32[1,1,8192]{2,1,0:T(1,128)S(1)} %bitcast.99), channel_id=1, replica_groups=mesh['ctx'=64,'cache'=4] {'cache'}, dimensions={0}, use_global_device_ids=true | all-gather | bytes 163840 | tf_op jit(solution)/shard_map/all_gather | solution.py:13
  349.6 129.3 %all-gather.2.cloned.1.call-done = f32[4,8192,1,128]{3,1,2,0:T(8,128)} async-done(((f32[1,8192,1,128]{3,1,2,0:T(8,128)}), f32[4,8192,1,128]{3,1,2,0:T(8,128)}) %all-gather.2.cloned.1.call-update) | async-done | bytes 16777232 | tf_op jit(solution)/shard_map/all_gather | solution.py:13
  478.9 4.4 dynamic_slice.65
  483.3 120.8 %while.36 = (s32[]{:T(128)}, f32[1,8192]{1,0:T(1,128)S(1)}, f32[1,8192]{1,0:T(1,128)S(1)}, f32[8192,1,128]{2,1,0:T(1,128)}, f32[4,1,8192]{2,1,0:T(1,128)S(1)}, /...) while((s32[]{:T(128)}, f32[1,8192]{1,0:T(1,128)S(1)}, ...), condition=%wide.region_6.7_spmd, body=%wide.region_5.6_spmd.sunk | while | flops 3194885 | bytes 54853828 | solution.py:18
  483.4 2.6 constant_dynamic-slice_fusion.6
  486.9 34.7 %multiply_add_fusion.5 = f32[8192,1,128]{2,1,0:T(1,128)S(1)} fusion(f32[8192,1,128]{2,1,0:T(1,128)S(1)} %bitcast.85, f32[8192,1,128]{2,1,0:T(1,128)S(1)} %copy-done.2, f32[8192]{0:T(1024)S(1)} %bitcast.97, f32[8192]{0:T(1024)S(1)} %bitcast.96), kind=kLoop, calls=%fused_computation.3.clone.1 | loop fusion | flops 3145728 | bytes 12648448 | tf_op jit(solution)/shard_map/while/body/eval_jaxpr/add | solution.py:78
  521.6 1.9 copy-done.3
  523.7 2.6 constant_dynamic-slice_fusion.6
  527.1 34.7 %multiply_add_fusion.5 = f32[8192,1,128]{2,1,0:T(1,128)S(1)} fusion(f32[8192,1,128]{2,1,0:T(1,128)S(1)} %bitcast.85, f32[8192,1,128]{2,1,0:T(1,128)S(1)} %copy-done.2, f32[8192]{0:T(1024)S(1)} %bitcast.97, f32[8192]{0:T(1024)S(1)} %bitcast.96), kind=kLoop, calls=%fused_computation.3.clone.1 | loop fusion | flops 3145728 | bytes 12648448 | tf_op jit(solution)/shard_map/while/body/eval_jaxpr/add | solution.py:78
  561.9 1.9 copy-done.3
  564.0 2.6 constant_dynamic-slice_fusion.6
  567.4 34.7 %multiply_add_fusion.5 = f32[8192,1,128]{2,1,0:T(1,128)S(1)} fusion(f32[8192,1,128]{2,1,0:T(1,128)S(1)} %bitcast.85, f32[8192,1,128]{2,1,0:T(1,128)S(1)} %copy-done.2, f32[8192]{0:T(1024)S(1)} %bitcast.97, f32[8192]{0:T(1024)S(1)} %bitcast.96), kind=kLoop, calls=%fused_computation.3.clone.1 | loop fusion | flops 3145728 | bytes 12648448 | tf_op jit(solution)/shard_map/while/body/eval_jaxpr/add | solution.py:78
  602.1 1.9 copy-done.3
  604.1 2.9 divide_convert_fusion
  607.0 61.3 %all_to_all.38 = bf16[64,128,128]{2,1,0:T(8,128)(2,1)} all-to-all(bf16[64,128,128]{2,1,0:T(8,128)(2,1)S(1)} %bitcast.92), channel_id=1, replica_groups=mesh['ctx'=64,'cache'=4] {'ctx'}, dimensions={0} | all-to-all | bytes 4194304 | tf_op jit(solution)/shard_map/all_to_all | solution.py:121
  668.3 4.1 copy.51
  672.3 4.1 copy.52
  (425 shorter events, 177.5 us)
Async XLA Ops:
  6.5 1.6 copy-start
  10.0 12.4 %copy-start.7 = (s32[32,16]{0,1:T(8,128)S(1)}, s32[32,16]{0,1:T(8,128)}, u32[]{:S(2)}) copy-start(s32[32,16]{0,1:T(8,128)} %param.13) | copy-start | bytes 6148
  10.0 63.3 %copy-start.1 = (s32[192]{0:T(256)S(1)}, s32[192]{0:T(256)}, u32[]{:S(2)}) copy-start(s32[192]{0:T(256)} %param.14) | copy-start | bytes 2308
  10.0 63.3 %copy-start.6 = (s32[32]{0:T(128)S(1)}, s32[32]{0:T(128)}, u32[]{:S(2)}) copy-start(s32[32]{0:T(128)} %param.15) | copy-start | bytes 388
  10.0 63.3 %all-to-all-start = ((bf16[128,64,128]{2,0,1:T(8,128)(2,1)}), bf16[128,64,128]{2,0,1:T(8,128)(2,1)}, u32[]{:S(2)}, u32[]{:S(2)}) async-start(bf16[128,64,128]{2,0,1:T(8,128)(2,1)} %copy_bitcast_fusion), calls=%async_computation | async-start | bytes 4194304 | tf_op jit(solution)/shard_map/all_to_all | solution.py:85
  22.4 456.5 %all-gather.2.cloned.1.call-start = ((), (), s32[]{:S(2)}) async-start(), calls=%async_computation.2 | async-start | bytes 20971520 | tf_op jit(solution)/shard_map/all_gather | solution.py:13
  325.3 0.8 copy-start.5
  325.3 11.6 %copy-start.4 = (f32[16,2,1,256]{3,2,1,0:T(1,128)S(1)}, f32[16,2,1,256]{3,2,1,0:T(1,128)}, u32[]{:S(2)}) copy-start(f32[16,2,1,256]{3,2,1,0:T(1,128)} %get-tuple-element.335) | copy-start | bytes 98308
  483.4 3.4 copy-start.2
  521.6 1.9 copy-start.3
  523.7 3.4 copy-start.2
  561.9 1.9 copy-start.3
  563.9 3.4 copy-start.2
  602.1 1.9 copy-start.3
Sparse Core Ops, SparseCore 0:
  325.4 153.4 all-gather.1
where the time goes:
time: 689 us; the launch traced here: 683 us
  local copies, waits for them, and re-layouts  187 us (27%)
  waiting for transfers between devices  179 us (26%)
  other arithmetic  145 us (21%)
  blocking collectives  84.8 us (12%)
  matrix products  39.1 us (6%)
  loops' own time  22 us (3%)
  between operations  13.5 us (2%)
  starting transfers between devices  12.4 us (2%)
    all_gather x1, waiting for transfers between devices, merged(): gathered = jax.tree.map(lambda a: lax.all_gather(a, axis), part)  129 us
    add x3, other arithmetic, combine(): numer_left * jnp.transpose(left_scale)[:, :, None]  104 us
    all_to_all x1, blocking collectives, shards(): lax.all_to_all(head_output, 'ctx', split_axis=0, concat_axis=1, tiled=True)  61.3 us
    all_to_all x1, waiting for transfers between devices, shards(): lax.all_to_all(queries, 'ctx', split_axis=1, concat_axis=0, tiled=True)  50.2 us
    gather x16, local copies, waits for them, and re-layouts, attend(): key_cache[safe_local]  40.6 us
    dynamic_update_slice x64, local copies, waits for them, and re-layouts, shards(): lax.map(one_step, jnp.arange(step_count, dtype=jnp.int32))  32.2 us
    gather x16, local copies, waits for them, and re-layouts, attend(): value_cache[safe_local]  28.5 us
    dot_general x16, matrix products, attend(): jnp.einsum('gthd,gkhd->ghtk', query_blocks, key_rows, preferred_element_t...  26.2 us
  transfers between devices with their start and end apart: 2, of which 2 were waited for; matrix products, arithmetic and copies ran while one was open for 0% of the time, Pallas kernels for 0%

commit v1 on v0

v1 whole, which is shorter than its diff:
```python
import jax
import jax.numpy as jnp
from jax import lax
from jax.experimental import pallas as pl
from jax.experimental.pallas import tpu as pltpu
from jax.sharding import PartitionSpec as P

HD = 128
BLOCK = 256
GROUP = 4
FAR = 1e30
SCALE2 = HD ** (-0.5) * 1.4426950408889634


def partial_kernel(unroll, lists, owners, starts, q, k, v, out, lse, picked, tops, totals, sums):
    held, lat, _ = k.shape
    images = owners.shape[0]
    requests = starts.shape[0]
    tokens = q.shape[0]
    slots = lists.shape[1] // 2
    first = lax.axis_index("cache") * held
    wide = BLOCK + HD

    def pick(u, r):
        count = jnp.int32(0)
        for s in range(slots):
            picked[u, s] = 0
        for s in range(slots):
            image = lists[r, slots + s]
            local = image - first
            owner = owners[jnp.minimum(image, images - 1)]
            here = (image < images) & (owner == r) & (local >= 0) & (local < held)
            picked[u, count] = jnp.where(here, local, 0)
            count = count + here.astype(jnp.int32)
        return count

    def window(r):
        low = pl.multiple_of(r * BLOCK, BLOCK)
        high = pl.multiple_of(jnp.minimum(low + BLOCK, tokens - HD), HD)
        return jnp.concatenate([q[pl.ds(low, BLOCK), :], q[pl.ds(high, HD), :]], axis=0)

    def chunk(u, r, base, count):
        rows = window(r)
        ids = [picked[u, base + s] for s in range(GROUP)]
        keys = jnp.concatenate([k[i] for i in ids], axis=0)
        scores = lax.dot_general(
            keys, rows, (((1,), (1,)), ((), ())), preferred_element_type=jnp.float32
        )
        parts = [scores[s * lat : (s + 1) * lat] for s in range(GROUP)]
        top = jnp.full((1, wide), -FAR, jnp.float32)
        for s in range(GROUP):
            here = jnp.max(parts[s], axis=0, keepdims=True)
            top = jnp.maximum(top, jnp.where(base + s < count, here, -FAR))
        top = jnp.where(base < count, top, 0.0)
        probs = []
        total = jnp.zeros((1, wide), jnp.float32)
        for s in range(GROUP):
            level = top + jnp.where(base + s < count, 0.0, FAR)
            p = jnp.exp2((parts[s] - level) * SCALE2)
            total = total + jnp.sum(p, axis=0, keepdims=True)
            probs.append(p.astype(jnp.bfloat16))
        vals = jnp.concatenate([v[i] for i in ids], axis=0)
        summed = lax.dot_general(
            vals,
            jnp.concatenate(probs, axis=0),
            (((0,), (0,)), ((), ())),
            preferred_element_type=jnp.float32,
        )
        return top, total, summed

    def step(g, carry):
        counts = []
        for u in range(unroll):
            counts.append(pick(u, g * unroll + u))
        for u in range(unroll):
            tops[u], totals[u], sums[u] = chunk(u, g * unroll + u, 0, counts[u])
        for u in range(unroll):

            @pl.when(counts[u] > GROUP)
            def _():
                top1, total1, sum1 = chunk(u, g * unroll + u, GROUP, counts[u])
                top0 = tops[u]
                both = jnp.maximum(top0, top1)
                scale0 = jnp.exp2((top0 - both) * SCALE2)
                scale1 = jnp.exp2((top1 - both) * SCALE2)
                tops[u] = both
                totals[u] = totals[u] * scale0 + total1 * scale1
                sums[u] = sums[u] * scale0 + sum1 * scale1

        for u in range(unroll):
            r = g * unroll + u
            total = totals[u]
            seen = total > 0
            safe = jnp.where(seen, total, 1.0)
            level = jnp.where(seen, tops[u] * SCALE2 + jnp.log2(safe), -FAR)
            result = (sums[u] * (1.0 / safe)).astype(jnp.bfloat16)
            low = pl.multiple_of(r * BLOCK, BLOCK)
            position = low + lax.broadcasted_iota(jnp.int32, (1, HD), 1)
            mine = position >= starts[r]
            lse[:, pl.ds(low, HD)] = jnp.where(mine, level[:, :HD], lse[:, pl.ds(low, HD)])
            old = out[:, pl.ds(low, HD)].astype(jnp.float32)
            new = result[:, :HD].astype(jnp.float32)
            out[:, pl.ds(low, HD)] = jnp.where(mine, new, old).astype(jnp.bfloat16)
            mid = pl.multiple_of(low + HD, HD)
            lse[:, pl.ds(mid, HD)] = level[:, HD:BLOCK]
            out[:, pl.ds(mid, HD)] = result[:, HD:BLOCK]

            @pl.when(r < requests - 1)
            def _():
                high = pl.multiple_of(low + BLOCK, HD)
                lse[:, pl.ds(high, HD)] = level[:, BLOCK:]
                out[:, pl.ds(high, HD)] = result[:, BLOCK:]

        return carry

    lax.fori_loop(0, requests // unroll, step, 0)


def partial_attention(q, k, v, block_imgs, img_req, req_start):
    tokens = q.shape[0]
    unroll = 2
    wide = BLOCK + HD
    smem = pl.BlockSpec(memory_space=pltpu.SMEM)
    vmem = pl.BlockSpec(memory_space=pltpu.VMEM)

    def kernel(*refs):
        partial_kernel(unroll, *refs)

    return pl.pallas_call(
        kernel,
        out_shape=(
            jax.ShapeDtypeStruct((HD, tokens), jnp.bfloat16),
            jax.ShapeDtypeStruct((1, tokens), jnp.float32),
        ),
        in_specs=[smem, smem, smem, vmem, vmem, vmem],
        out_specs=(vmem, vmem),
        scratch_shapes=[
            pltpu.SMEM((unroll, 16), jnp.int32),
            pltpu.VMEM((unroll, 1, wide), jnp.float32),
            pltpu.VMEM((unroll, 1, wide), jnp.float32),
            pltpu.VMEM((unroll, HD, wide), jnp.float32),
        ],
        name="partial",
    )(block_imgs, img_req, req_start, q, k, v)


def shards(queries, keys, values, block_imgs, img_req, req_start):
    ctx = lax.axis_size("ctx")
    cache = lax.axis_size("cache")
    me = lax.axis_index("cache")
    rows = queries.shape[0]
    part = rows // cache
    tokens = rows * ctx
    quarter = lax.dynamic_slice_in_dim(queries, me * part, part, 0)
    spread = lax.all_to_all(quarter, "ctx", split_axis=1, concat_axis=0, tiled=True)
    gathered = lax.all_gather(spread.reshape(ctx, part, HD), "cache")
    q = jnp.transpose(gathered, (1, 0, 2, 3)).reshape(tokens, HD)
    out, lse = partial_attention(q, keys, values, block_imgs, img_req, req_start)
    deep = HD // cache
    parts = lax.all_to_all(out.reshape(cache, deep, tokens), "cache", 0, 0)
    levels = lax.all_gather(lse, "cache")
    top = jnp.max(levels, axis=0)
    weights = jnp.exp2(levels - top)
    merged = jnp.sum(parts.astype(jnp.float32) * weights, axis=0) / jnp.sum(weights, axis=0)
    merged = merged.astype(jnp.bfloat16)
    mine = lax.all_to_all(
        jnp.transpose(merged.reshape(deep, ctx, rows), (1, 0, 2)), "ctx", 0, 0
    )
    every = lax.all_gather(mine, "cache")
    return jnp.transpose(every, (3, 1, 0, 2)).reshape(rows, ctx * HD)


def solution(mesh):
    placed = (P("ctx", None), P("cache", None, "ctx"), P("cache", None, "ctx"), P(), P(), P())
    return jax.shard_map(
        shards, mesh=mesh, in_specs=placed, out_specs=P("ctx", None), check_vma=False
    )
```

time: 689 us -> 202 us (0.29)
  local copies, waits for them, and re-layouts: 187 us -> 14.2 us
  other arithmetic: 145 us -> 2.71 us
  waiting for transfers between devices: 179 us -> 59.3 us
  matrix products: 39.1 us -> 0 us
  loops' own time: 22 us -> 0 us
  Pallas kernels: 0 us -> 17.4 us
    add x38 -> x0, other arithmetic: 106 us -> none  [the longest x3 104 us: combine(): numer_left * jnp.transpose(left_scale)[:, :, None]]
    gather x64 -> x0, local copies, waits for them, and re-layouts: 81.9 us -> none  [the longest x16 40.6 us: attend(): key_cache[safe_local]]
    all_gather x1 -> x2, waiting for transfers between devices: 129 us -> 59.3 us  [the longest x1 30.3 us: shards(): every = lax.all_gather(mine, 'cache')]
    all_to_all x1, waiting for transfers between devices: 50.2 us -> 0.01 us  [shards(): parts = lax.all_to_all(out.reshape(cache, deep, tokens), 'cache', 0, 0)]
    dot_general x32 -> x0, matrix products: 39.1 us -> none  [the longest x16 26.2 us: attend(): jnp.einsum('gthd,gkhd->ghtk', query_blocks, key_rows, preferred_element_t...]
    dynamic_slice x36 -> x0, local copies, waits for them, and re-layouts: 36.3 us -> none  [the longest x16 14.7 us: one_step(): lax.dynamic_slice_in_dim(head_rows, step_index * group_size * block_len,...]
    dynamic_update_slice x64 -> x0, local copies, waits for them, and re-layouts: 32.2 us -> none  [shards(): lax.map(one_step, jnp.arange(step_count, dtype=jnp.int32))]
    another operation x2 -> x0, loops' own time: 22 us -> none  [the longest x1 22 us: shards(): lax.map(one_step, jnp.arange(step_count, dtype=jnp.int32))]
  transfers between devices with their start and end apart: 2 -> 3, of which waited for: 2 -> 2; matrix products, arithmetic and copies ran while one was open for 0% -> 1% of each run, Pallas kernels for 0% -> 0%
where the time goes in v1:
time: 202 us; the launch traced here: 199 us
  blocking collectives  85.9 us (43%)
  waiting for transfers between devices  59.3 us (29%)
  Pallas kernels  17.4 us (9%)
  local copies, waits for them, and re-layouts  14.2 us (7%)
  between operations  13.5 us (7%)
  starting transfers between devices  6.32 us (3%)
  other arithmetic  2.71 us (1%)
    all_gather x1, waiting for transfers between devices, shards(): every = lax.all_gather(mine, 'cache')  30.3 us
    all_gather x1, blocking collectives, shards(): levels = lax.all_gather(lse, 'cache')  29.6 us
    all_gather x1, waiting for transfers between devices, shards(): gathered = lax.all_gather(spread.reshape(ctx, part, HD), 'cache')  28.9 us
    all_to_all x1, blocking collectives, shards(): lax.all_to_all(quarter, 'ctx', split_axis=1, concat_axis=0, tiled=True)  28.9 us
    all_to_all x1, blocking collectives, shards(): lax.all_to_all(jnp.transpose(merged.reshape(deep, ctx, rows), (1, 0, 2)),...  27.4 us
    pallas_call x1, Pallas kernels, partial_attention(): pl.pallas_call(kernel, out_shape=(jax.ShapeDtypeStruct((HD, tokens), jnp....  17.4 us
    all_to_all x1, starting transfers between devices, shards(): parts = lax.all_to_all(out.reshape(cache, deep, tokens), 'cache', 0, 0)  6.32 us
    reshape x1, local copies, waits for them, and re-layouts, shards(): return jnp.transpose(every, (3, 1, 0, 2)).reshape(rows, ctx * HD)  4.06 us
  transfers between devices with their start and end apart: 3, of which 2 were waited for; matrix products, arithmetic and copies ran while one was open for 1% of the time, Pallas kernels for 0%

profile of v1, /device:TPU:16, one launch (start us, length us, event | category | flops | bytes accessed | tf_op | source)
XLA Modules:
  0.0 199.2 jit_solution(7366110378928131497)
XLA Ops:
  6.5 0.0 copy-start
  6.5 0.0 copy-start.2
  6.5 0.0 all-gather.7.cloned.1.call-start
  6.5 1.6 copy-done
  8.1 0.1 copy_bitcast_fusion
  8.2 28.9 %all_to_all.26 = bf16[32,64,128]{2,0,1:T(8,128)(2,1)} all-to-all(bf16[32,64,128]{2,0,1:T(8,128)(2,1)S(1)} %copy_bitcast_fusion), channel_id=1, replica_groups=mesh['ctx'=64,'cache'=4] {'ctx'}, dimensions={1} | all-to-all | bytes 1048576 | tf_op jit(solution)/shard_map/all_to_all | solution.py:155
  37.1 0.0 all-gather.7.cloned.1.call-update
  37.1 0.0 copy-done.2
  37.1 0.7 copy.26.refs_0_
  37.8 28.9 %all-gather.7.cloned.1.call-done = bf16[256,32,128]{2,1,0:T(8,128)(2,1)} async-done(((bf16[64,32,128]{2,1,0:T(8,128)(2,1)}), bf16[256,32,128]{2,1,0:T(8,128)(2,1)}) %all-gather.7.cloned.1.call-update) | async-done | bytes 2097168 | tf_op jit(solution)/shard_map/all_gather | solution.py:156
  66.8 3.6 %copy.25 = bf16[64,4,32,128]{3,2,1,0:T(8,128)(2,1)} copy(bf16[64,4,32,128]{3,2,0,1:T(8,128)(2,1)} %bitcast.31) | data formatting | bytes 4194304 | tf_op jit(solution)/shard_map/transpose | solution.py:157
  70.3 17.4 %partial.1 = (bf16[128,8192]{1,0:T(8,128)(2,1)}, f32[1,8192]{1,0:T(1,128)}) custom-call(s32[32,16]{1,0:T(8,128)} %copy.26.refs_0_, s32[192]{0:T(256)} %refs_1_.1, s32[32]{0:T(128)} %refs_2_.1, bf16[8192,128]{1,0:T(8,128)(2,1)} %bitcast.26, bf16[48,64,128]{2,1,0:T(8,128)(2,1)} %refs_4_.1, bf16[48,64,128]{2,1,0:T(8,128)(2,1)} %refs_5_.1), custom_call_target="tpu_custom_call" | custom-call | tf_op jit(solution)/shard_map/partial/pallas_call | solution.py:129
  87.7 0.0 copy-start.1
  87.7 6.3 %all-to-all-start.1 = ((bf16[4,32,8192]{2,1,0:T(8,128)(2,1)}), bf16[4,32,8192]{2,1,0:T(8,128)(2,1)}, u32[]{:S(2)}, u32[]{:S(2)}) async-start(bf16[4,32,8192]{2,1,0:T(8,128)(2,1)} %bitcast.30), calls=%async_computation.1 | async-start | bytes 4194304 | tf_op jit(solution)/shard_map/all_to_all | solution.py:160
  94.0 0.0 all-gather.9.cloned.1.call-start
  94.0 0.0 copy-done.1
  94.0 29.6 %all-gather.3 = f32[4,1,8192]{2,1,0:T(1,128)S(1)} all-gather(f32[1,1,8192]{2,1,0:T(1,128)S(1)} %bitcast.36), channel_id=3, replica_groups=mesh['ctx'=64,'cache'=4] {'cache'}, dimensions={0}, use_global_device_ids=true | all-gather | bytes 163840 | tf_op jit(solution)/shard_map/all_gather | solution.py:161
  123.6 0.1 reduce_max.9
  123.8 0.3 fusion.1
  124.1 0.1 copy.35
  124.2 0.0 all-to-all-done.1
  124.2 2.2 %multiply_reduce_fusion = f32[32,8192]{1,0:T(8,128)S(1)} fusion(bf16[4,32,8192]{2,1,0:T(8,128)(2,1)} %all-to-all-done.1, f32[4,8192]{1,0:T(4,128)S(1)} %bitcast.34), kind=kLoop, calls=%fused_computation | loop fusion | flops 2883584 | bytes 3276800 | tf_op jit(solution)/shard_map/reduce_sum | solution.py:164
  126.3 0.2 copy.32
  126.5 0.1 fusion
  126.7 0.3 copy.27
  127.0 27.4 %all_to_all.27 = bf16[64,32,128]{2,1,0:T(8,128)(2,1)} all-to-all(bf16[64,32,128]{2,1,0:T(8,128)(2,1)S(1)} %copy.27), channel_id=1, replica_groups=mesh['ctx'=64,'cache'=4] {'ctx'}, dimensions={0} | all-to-all | bytes 1048576 | tf_op jit(solution)/shard_map/all_to_all | solution.py:166
  154.4 0.0 all-gather.9.cloned.1.call-update
  154.4 30.3 %all-gather.9.cloned.1.call-done = bf16[256,32,128]{2,1,0:T(8,128)(2,1)} async-done(((bf16[64,32,128]{2,1,0:T(8,128)(2,1)}), bf16[256,32,128]{2,1,0:T(8,128)(2,1)}) %all-gather.9.cloned.1.call-update) | async-done | bytes 2097168 | tf_op jit(solution)/shard_map/all_gather | solution.py:169
  184.7 3.5 %copy.28 = bf16[128,64,4,32]{0,3,2,1:T(8,128)(2,1)} copy(bf16[128,64,4,32]{0,3,1,2:T(8,128)(2,1)} %bitcast.32) | data formatting | bytes 4194304 | tf_op jit(solution)/shard_map/transpose | solution.py:170
  188.3 4.1 %copy.29 = bf16[128,8192]{1,0:T(8,128)(2,1)} copy(bf16[128,8192]{0,1:T(8,128)(2,1)} %bitcast.27) | data formatting | bytes 4194304 | tf_op jit(solution)/shard_map/reshape | solution.py:170
Async XLA Ops:
  6.5 1.6 copy-start
  6.5 30.6 %copy-start.2 = (s32[32,16]{0,1:T(8,128)S(1)}, s32[32,16]{0,1:T(8,128)}, u32[]{:S(2)}) copy-start(s32[32,16]{0,1:T(8,128)} %param.9) | copy-start | bytes 6148
  6.5 60.2 %all-gather.7.cloned.1.call-start = ((), (), s32[]{:S(2)}) async-start(), calls=%async_computation.3 | async-start | bytes 2621440 | tf_op jit(solution)/shard_map/all_gather | solution.py:156
  87.7 6.3 %copy-start.1 = (f32[1,8192]{1,0:T(1,128)S(1)}, f32[1,8192]{1,0:T(1,128)}, u32[]{:S(2)}) copy-start(f32[1,8192]{1,0:T(1,128)} %get-tuple-element.8) | copy-start | bytes 98308
  87.7 36.5 %all-to-all-start.1 = ((bf16[4,32,8192]{2,1,0:T(8,128)(2,1)}), bf16[4,32,8192]{2,1,0:T(8,128)(2,1)}, u32[]{:S(2)}, u32[]{:S(2)}) async-start(bf16[4,32,8192]{2,1,0:T(8,128)(2,1)} %bitcast.30), calls=%async_computation.1 | async-start | bytes 4194304 | tf_op jit(solution)/shard_map/all_to_all | solution.py:160
  94.0 90.7 %all-gather.9.cloned.1.call-start = ((), (), s32[]{:S(2)}) async-start(), calls=%async_computation.4 | async-start | bytes 2621440 | tf_op jit(solution)/shard_map/all_gather | solution.py:169
Sparse Core Ops, SparseCore 0:
  37.3 29.4 all-gather.6
  154.6 30.1 all-gather.8

commit v2 on v1

--- a/solution.py
+++ b/solution.py
@@ -144,17 +144,156 @@
     )(block_imgs, img_req, req_start, q, k, v)
 
 
+NX = 4
+NZ = 8
+MESH = pl.DeviceIdType.MESH
+
+
+def push(src, dst, sent, landed, ctx, cache):
+    return pltpu.make_async_remote_copy(
+        src_ref=src,
+        dst_ref=dst,
+        send_sem=sent,
+        recv_sem=landed,
+        device_id=(ctx, cache),
+        device_id_type=MESH,
+    )
+
+
+def turn(i):
+    return 0 if i == 0 else ((i + 1) // 2 if i % 2 else NZ - i // 2)
+
+
+def place():
+    c = lax.axis_index("ctx")
+    y = lax.axis_index("cache")
+    return c, y, c // (2 * NZ), lax.rem(c // 2, NZ), lax.rem(c, 2)
+
+
+def greet(c, y, offsets):
+    barrier = pltpu.get_barrier_semaphore()
+
+    def ring(s, carry):
+        pl.semaphore_signal(
+            barrier, inc=1, device_id=(lax.rem(c + s, 2 * NX * NZ), y), device_id_type=MESH
+        )
+        return carry
+
+    lax.fori_loop(1, 2 * NX * NZ, ring, 0)
+    for o in offsets:
+        pl.semaphore_signal(
+            barrier, inc=1, device_id=(c, lax.rem(y + o, 4)), device_id_type=MESH
+        )
+    pl.semaphore_wait(barrier, 2 * NX * NZ - 1 + len(offsets))
+
+
+def share(buf, sems, c, y, z, part):
+    sent, came, left, right, far = sems
+    up = lax.rem(y + 1, 4)
+    down = lax.rem(y + 3, 4)
+
+    def piece(dz, who):
+        return buf.at[:, lax.rem(z + NZ - dz, NZ), :, pl.ds(who * part, part), :]
+
+    def forward(i):
+        dz = turn(i)
+        own = piece(dz, y)
+        push(own, own, sent.at[0, dz], came.at[dz], c, up).wait_recv()
+        push(own, own, sent.at[0, dz], left.at[dz], c, up).start()
+        push(own, own, sent.at[1, dz], right.at[dz], c, down).start()
+
+    def relay(i):
+        dz = turn(i)
+        if i % 2 == 0:
+            got = piece(dz, down)
+            push(got, got, sent.at[2, dz], left.at[dz], c, up).wait_recv()
+            push(got, got, sent.at[2, dz], far.at[dz], c, up).start()
+        else:
+            got = piece(dz, up)
+            push(got, got, sent.at[2, dz], right.at[dz], c, down).wait_recv()
+            push(got, got, sent.at[2, dz], far.at[dz], c, down).start()
+
+    def finish(i):
+        dz = turn(i)
+        if i % 2 == 0:
+            got = piece(dz, up)
+            push(got, got, sent.at[2, dz], right.at[dz], c, down).wait_recv()
+        else:
+            got = piece(dz, down)
+            push(got, got, sent.at[2, dz], left.at[dz], c, up).wait_recv()
+        got = piece(dz, lax.rem(y + 2, 4))
+        push(got, got, sent.at[2, dz], far.at[dz], c, up).wait_recv()
+        own = piece(dz, y)
+        for k in range(3):
+            push(own, own, sent.at[k, dz], far.at[dz], c, up).wait_send()
+
+    return forward, relay, finish
+
+
+def spread_kernel(part, q, buf, out_sem, sent, came, left, right, far):
+    c, y, x, z, core = place()
+    greet(c, y, (1, 3))
+    rows = pl.ds(y * part, part)
+    mine = buf.at[x, z, core, rows, :]
+
+    def block(to):
+        return q.at[rows, pl.ds(pl.multiple_of(to * HD, HD), HD)]
+
+    for i in range(NZ):
+        dz = turn(i)
+
+        def send(j, carry):
+            to = (
+                lax.rem(x + j // 2, NX) * (2 * NZ)
+                + lax.rem(z + dz, NZ) * 2
+                + lax.rem(core + lax.rem(j, 2), 2)
+            )
+            push(block(to), mine, out_sem.at[dz], came.at[dz], to, y).start()
+            return carry
+
+        if i == 0:
+            pltpu.make_async_copy(block(c), mine, came.at[0]).start()
+        lax.fori_loop(1 if i == 0 else 0, 2 * NX, send, 0)
+    forward, relay, finish = share(buf, (sent, came, left, right, far), c, y, z, part)
+    for i in range(NZ + 1):
+        if i < NZ:
+            forward(i)
+        if i >= 1:
+            relay(i - 1)
+    for i in range(NZ):
+        dz = turn(i)
+        finish(i)
+        whole = buf.at[:, z, :, rows, :]
+        if i == 0:
+            some = q.at[rows, pl.ds(0, (2 * NX - 1) * HD)]
+            push(some, some, out_sem.at[dz], came.at[dz], c, y).wait_send()
+        else:
+            push(whole, whole, out_sem.at[dz], came.at[dz], c, y).wait_send()
+
+
+def spread(queries, part):
+    def kernel(*refs):
+        spread_kernel(part, *refs)
+
+    dma = pltpu.SemaphoreType.DMA
+    return pl.pallas_call(
+        kernel,
+        out_shape=jax.ShapeDtypeStruct((NX, NZ, 2, 4 * part, HD), jnp.bfloat16),
+        in_specs=[pl.BlockSpec(memory_space=pl.ANY)],
+        out_specs=pl.BlockSpec(memory_space=pltpu.VMEM),
+        scratch_shapes=[dma((NZ,)), dma((3, NZ)), dma((NZ,)), dma((NZ,)), dma((NZ,)), dma((NZ,))],
+        compiler_params=pltpu.CompilerParams(collective_id=1, has_side_effects=True),
+        name="spread",
+    )(queries)
+
+
 def shards(queries, keys, values, block_imgs, img_req, req_start):
     ctx = lax.axis_size("ctx")
     cache = lax.axis_size("cache")
-    me = lax.axis_index("cache")
     rows = queries.shape[0]
     part = rows // cache
     tokens = rows * ctx
-    quarter = lax.dynamic_slice_in_dim(queries, me * part, part, 0)
-    spread = lax.all_to_all(quarter, "ctx", split_axis=1, concat_axis=0, tiled=True)
-    gathered = lax.all_gather(spread.reshape(ctx, part, HD), "cache")
-    q = jnp.transpose(gathered, (1, 0, 2, 3)).reshape(tokens, HD)
+    q = spread(queries, part).reshape(tokens, HD)
     out, lse = partial_attention(q, keys, values, block_imgs, img_req, req_start)
     deep = HD // cache
     parts = lax.all_to_all(out.reshape(cache, deep, tokens), "cache", 0, 0)

time: 202 us -> 167 us (0.83)
  Pallas kernels: 17.4 us -> 57.5 us
  blocking collectives: 85.9 us -> 49.9 us
  waiting for transfers between devices: 59.3 us -> 30.2 us
  local copies, waits for them, and re-layouts: 14.2 us -> 7.12 us
    pallas_call x0 -> x1, Pallas kernels: none -> 40.6 us  [spread(): pl.pallas_call(kernel, out_shape=jax.ShapeDtypeStruct((NX, NZ, 2, 4 * par...]
    all_gather x1 -> x0, waiting for transfers between devices: 28.9 us -> none  [shards(): gathered = lax.all_gather(spread.reshape(ctx, part, HD), 'cache')]
    all_to_all x1 -> x0, blocking collectives: 28.9 us -> none  [shards(): lax.all_to_all(quarter, 'ctx', split_axis=1, concat_axis=0, tiled=True)]
    all_to_all x1, blocking collectives: 27.4 us -> 23.1 us  [shards(): lax.all_to_all(jnp.transpose(merged.reshape(deep, ctx, rows), (1, 0, 2)),...]
    transpose x1 -> x0, local copies, waits for them, and re-layouts: 3.56 us -> none  [shards(): q = jnp.transpose(gathered, (1, 0, 2, 3)).reshape(tokens, HD)]
    all_gather x1, blocking collectives: 29.6 us -> 26.8 us  [shards(): levels = lax.all_gather(lse, 'cache')]
  transfers between devices with their start and end apart: 3 -> 2, of which waited for: 2 -> 1; matrix products, arithmetic and copies ran while one was open for 1% -> 0% of each run, Pallas kernels for 0% -> 0%
where the time goes in v2:
time: 167 us; the launch traced here: 165 us
  Pallas kernels  57.5 us (34%)
  blocking collectives  49.9 us (30%)
  waiting for transfers between devices  30.2 us (18%)
  between operations  13.5 us (8%)
  local copies, waits for them, and re-layouts  7.12 us (4%)
  starting transfers between devices  5.29 us (3%)
    pallas_call x1, Pallas kernels, spread(): pl.pallas_call(kernel, out_shape=jax.ShapeDtypeStruct((NX, NZ, 2, 4 * par...  40.6 us
    all_gather x1, waiting for transfers between devices, shards(): every = lax.all_gather(mine, 'cache')  30.2 us
    all_gather x1, blocking collectives, shards(): levels = lax.all_gather(lse, 'cache')  26.8 us
    all_to_all x1, blocking collectives, shards(): lax.all_to_all(jnp.transpose(merged.reshape(deep, ctx, rows), (1, 0, 2)),...  23.1 us
    pallas_call x1, Pallas kernels, partial_attention(): pl.pallas_call(kernel, out_shape=(jax.ShapeDtypeStruct((HD, tokens), jnp....  16.9 us
    all_to_all x1, starting transfers between devices, shards(): parts = lax.all_to_all(out.reshape(cache, deep, tokens), 'cache', 0, 0)  5.29 us
  transfers between devices with their start and end apart: 2, of which 1 were waited for; matrix products, arithmetic and copies ran while one was open for 0% of the time, Pallas kernels for 0%

profile of v2, /device:TPU:16, one launch (start us, length us, event | category | flops | bytes accessed | tf_op | source)
XLA Modules:
  0.0 164.5 jit_solution(8018823151967119368)
XLA Ops:
  6.5 1.4 copy.19.refs_0_
  7.9 40.6 %spread.1 = bf16[4,8,2,128,128]{4,3,2,1,0:T(8,128)(2,1)} custom-call(bf16[128,8192]{1,0:T(8,128)(2,1)} %refs_0_.2), custom_call_target="tpu_custom_call" | custom-call | tf_op jit(solution)/shard_map/spread/pallas_call | solution.py:279
  48.5 16.9 %partial.1 = (bf16[128,8192]{1,0:T(8,128)(2,1)}, f32[1,8192]{1,0:T(1,128)}) custom-call(s32[32,16]{1,0:T(8,128)} %copy.19.refs_0_, s32[192]{0:T(256)} %refs_1_.1, s32[32]{0:T(128)} %refs_2_.1, bf16[8192,128]{1,0:T(8,128)(2,1)} %bitcast.17, bf16[48,64,128]{2,1,0:T(8,128)(2,1)} %refs_4_.1, bf16[48,64,128]{2,1,0:T(8,128)(2,1)} %refs_5_.1), custom_call_target="tpu_custom_call" | custom-call | tf_op jit(solution)/shard_map/partial/pallas_call | solution.py:129
  65.4 0.0 copy-start
  65.4 5.3 %all-to-all-start = ((bf16[4,32,8192]{2,1,0:T(8,128)(2,1)}), bf16[4,32,8192]{2,1,0:T(8,128)(2,1)S(1)}, u32[]{:S(2)}, u32[]{:S(2)}) async-start(bf16[4,32,8192]{2,1,0:T(8,128)(2,1)} %bitcast.21), calls=%async_computation | async-start | bytes 4194304 | tf_op jit(solution)/shard_map/all_to_all | solution.py:299
  70.7 0.0 all-gather.5.cloned.1.call-start
  70.7 0.0 copy-done
  70.7 26.8 %all-gather.2 = f32[4,1,8192]{2,1,0:T(1,128)S(1)} all-gather(f32[1,1,8192]{2,1,0:T(1,128)S(1)} %bitcast.25), channel_id=2, replica_groups=mesh['ctx'=64,'cache'=4] {'cache'}, dimensions={0}, use_global_device_ids=true | all-gather | bytes 163840 | tf_op jit(solution)/shard_map/all_gather | solution.py:300
  97.5 0.1 reduce_max.9
  97.6 0.3 fusion.1
  97.9 0.1 copy.26
  98.0 0.0 all-to-all-done
  98.0 0.4 multiply_reduce_fusion
  98.5 0.2 copy.24
  98.7 0.1 fusion
  98.8 0.3 copy.20
  99.2 23.1 %all_to_all.10 = bf16[64,32,128]{2,1,0:T(8,128)(2,1)} all-to-all(bf16[64,32,128]{2,1,0:T(8,128)(2,1)S(1)} %copy.20), channel_id=1, replica_groups=mesh['ctx'=64,'cache'=4] {'ctx'}, dimensions={0} | all-to-all | bytes 1048576 | tf_op jit(solution)/shard_map/all_to_all | solution.py:305
  122.3 0.0 all-gather.5.cloned.1.call-update
  122.3 30.2 %all-gather.5.cloned.1.call-done = bf16[256,32,128]{2,1,0:T(8,128)(2,1)} async-done(((bf16[64,32,128]{2,1,0:T(8,128)(2,1)}), bf16[256,32,128]{2,1,0:T(8,128)(2,1)}) %all-gather.5.cloned.1.call-update) | async-done | bytes 2097168 | tf_op jit(solution)/shard_map/all_gather | solution.py:308
  152.5 2.2 %copy.21 = bf16[128,64,4,32]{0,3,2,1:T(8,128)(2,1)S(1)} copy(bf16[128,64,4,32]{0,3,1,2:T(8,128)(2,1)} %bitcast.22) | data formatting | bytes 4194304 | tf_op jit(solution)/shard_map/transpose | solution.py:309
  154.8 2.9 %copy.22 = bf16[128,8192]{1,0:T(8,128)(2,1)} copy(bf16[128,8192]{0,1:T(8,128)(2,1)S(1)} %bitcast.18) | data formatting | bytes 4194304 | tf_op jit(solution)/shard_map/reshape | solution.py:309
Async XLA Ops:
  65.4 5.3 %copy-start = (f32[1,8192]{1,0:T(1,128)S(1)}, f32[1,8192]{1,0:T(1,128)}, u32[]{:S(2)}) copy-start(f32[1,8192]{1,0:T(1,128)} %get-tuple-element.8) | copy-start | bytes 98308
  65.4 32.6 %all-to-all-start = ((bf16[4,32,8192]{2,1,0:T(8,128)(2,1)}), bf16[4,32,8192]{2,1,0:T(8,128)(2,1)S(1)}, u32[]{:S(2)}, u32[]{:S(2)}) async-start(bf16[4,32,8192]{2,1,0:T(8,128)(2,1)} %bitcast.21), calls=%async_computation | async-start | bytes 4194304 | tf_op jit(solution)/shard_map/all_to_all | solution.py:299
  70.7 81.8 %all-gather.5.cloned.1.call-start = ((), (), s32[]{:S(2)}) async-start(), calls=%async_computation.2 | async-start | bytes 2621440 | tf_op jit(solution)/shard_map/all_gather | solution.py:308
Sparse Core Ops, SparseCore 0:
  122.4 30.0 all-gather.4

commit v3 on v2

--- a/solution.py
+++ b/solution.py
@@ -94,22 +94,19 @@
             safe = jnp.where(seen, total, 1.0)
             level = jnp.where(seen, tops[u] * SCALE2 + jnp.log2(safe), -FAR)
             result = (sums[u] * (1.0 / safe)).astype(jnp.bfloat16)
-            low = pl.multiple_of(r * BLOCK, BLOCK)
-            position = low + lax.broadcasted_iota(jnp.int32, (1, HD), 1)
+            position = r * BLOCK + lax.broadcasted_iota(jnp.int32, (1, HD), 1)
             mine = position >= starts[r]
-            lse[:, pl.ds(low, HD)] = jnp.where(mine, level[:, :HD], lse[:, pl.ds(low, HD)])
-            old = out[:, pl.ds(low, HD)].astype(jnp.float32)
+            lse[r, :, :HD] = jnp.where(mine, level[:, :HD], lse[r, :, :HD])
+            old = out[r, :, :HD].astype(jnp.float32)
             new = result[:, :HD].astype(jnp.float32)
-            out[:, pl.ds(low, HD)] = jnp.where(mine, new, old).astype(jnp.bfloat16)
-            mid = pl.multiple_of(low + HD, HD)
-            lse[:, pl.ds(mid, HD)] = level[:, HD:BLOCK]
-            out[:, pl.ds(mid, HD)] = result[:, HD:BLOCK]
+            out[r, :, :HD] = jnp.where(mine, new, old).astype(jnp.bfloat16)
+            lse[r, :, HD:] = level[:, HD:BLOCK]
+            out[r, :, HD:] = result[:, HD:BLOCK]
 
             @pl.when(r < requests - 1)
             def _():
-                high = pl.multiple_of(low + BLOCK, HD)
-                lse[:, pl.ds(high, HD)] = level[:, BLOCK:]
-                out[:, pl.ds(high, HD)] = result[:, BLOCK:]
+                lse[r + 1, :, :HD] = level[:, BLOCK:]
+                out[r + 1, :, :HD] = result[:, BLOCK:]
 
         return carry
 
@@ -129,8 +126,8 @@
     return pl.pallas_call(
         kernel,
         out_shape=(
-            jax.ShapeDtypeStruct((HD, tokens), jnp.bfloat16),
-            jax.ShapeDtypeStruct((1, tokens), jnp.float32),
+            jax.ShapeDtypeStruct((tokens // BLOCK, HD, BLOCK), jnp.bfloat16),
+            jax.ShapeDtypeStruct((tokens // BLOCK, 1, BLOCK), jnp.float32),
         ),
         in_specs=[smem, smem, smem, vmem, vmem, vmem],
         out_specs=(vmem, vmem),
@@ -287,6 +284,205 @@
     )(queries)
 
 
+def merge_kernel(
+    deep, part, lse, buf, levels, alpha, relayed, raw, added, adding, final,
+    lse_sent, lse_came, a_sent, a_came, r_sent, r_came, m_sent, m_came,
+    out_sem, came, sent, left, right, far,
+):
+    c, y, x, z, core = place()
+    up = lax.rem(y + 1, 4)
+    down = lax.rem(y + 3, 4)
+    across = lax.rem(y + 2, 4)
+    greet(c, y, (1, 2, 3))
+
+    def rows(who):
+        return pl.ds(pl.multiple_of(who * deep, deep), deep)
+
+    def chip(i):
+        return lax.rem(z + turn(i), NZ)
+
+    own_lse = pltpu.make_async_copy(lse, levels.at[y], lse_came.at[3])
+    own_lse.start()
+    tell = [
+        push(lse, levels.at[y], lse_sent.at[o - 1], lse_came.at[o - 1], c, lax.rem(y + o, 4))
+        for o in (1, 2, 3)
+    ]
+    for t in tell:
+        t.start()
+
+    def offers(i):
+        zs = chip(i)
+        return (
+            push(part.at[pl.ds(0, 2), zs, rows(across), :], relayed.at[0, i],
+                 a_sent.at[0, i], a_came.at[0, i], c, up),
+            push(part.at[pl.ds(2, 2), zs, rows(across), :], relayed.at[1, i],
+                 a_sent.at[1, i], a_came.at[1, i], c, down),
+            push(part.at[pl.ds(2, 2), zs, rows(up), :], raw.at[0, i],
+                 r_sent.at[0, i], r_came.at[0, i], c, up),
+            push(part.at[pl.ds(0, 2), zs, rows(down), :], raw.at[1, i],
+                 r_sent.at[1, i], r_came.at[1, i], c, down),
+        )
+
+    offered = [offers(i) for i in range(NZ)]
+
+    def offer(i):
+        for p in offered[i]:
+            p.start()
+
+    def adds(i):
+        return (
+            push(adding.at[0, i], added.at[0, i], m_sent.at[0, i], m_came.at[0, i], c, up),
+            push(adding.at[1, i], added.at[1, i], m_sent.at[1, i], m_came.at[1, i], c, down),
+        )
+
+    added_to = [adds(i) for i in range(NZ)]
+
+    def weigh(who, k, zs, block):
+        return block.astype(jnp.float32) * alpha[who, k * NZ + zs]
+
+    def add(i):
+        zs = chip(i)
+        ready = offered[i]
+        ready[0].wait_recv()
+        ready[1].wait_recv()
+        for k in range(2):
+            adding[0, i, k] = (
+                weigh(down, k, zs, relayed[0, i, k]) + weigh(y, k, zs, part[k, zs, rows(up), :])
+            ).astype(jnp.bfloat16)
+            adding[1, i, k] = (
+                weigh(up, k + 2, zs, relayed[1, i, k])
+                + weigh(y, k + 2, zs, part[k + 2, zs, rows(down), :])
+            ).astype(jnp.bfloat16)
+
+    def complete(i):
+        zs = chip(i)
+        ready = offered[i]
+        ready[2].wait_recv()
+        ready[3].wait_recv()
+        for p in added_to[i]:
+            p.wait_recv()
+        for k in range(2):
+            final[i, k] = (
+                weigh(y, k, zs, part[k, zs, rows(y), :])
+                + added[0, i, k].astype(jnp.float32)
+                + weigh(up, k, zs, raw[1, i, k])
+            ).astype(jnp.bfloat16)
+            final[i, k + 2] = (
+                weigh(y, k + 2, zs, part[k + 2, zs, rows(y), :])
+                + added[1, i, k].astype(jnp.float32)
+                + weigh(down, k + 2, zs, raw[0, i, k])
+            ).astype(jnp.bfloat16)
+
+    mine = buf.at[x, z, core, pl.ds(y * deep, deep), :]
+
+    def scatter(i):
+        dz = turn(i)
+        zs = chip(i)
+
+        def block(to_x, to_core):
+            return final.at[i, to_x, :, pl.ds(pl.multiple_of(to_core * HD, HD), HD)]
+
+        def send(j, carry):
+            to_x = lax.rem(x + j // 2, NX)
+            to_core = lax.rem(core + lax.rem(j, 2), 2)
+            to = to_x * (2 * NZ) + zs * 2 + to_core
+            push(block(to_x, to_core), mine, out_sem.at[dz], came.at[dz], to, y).start()
+            return carry
+
+        if i == 0:
+            pltpu.make_async_copy(block(x, core), mine, came.at[0]).start()
+        lax.fori_loop(1 if i == 0 else 0, 2 * NX, send, 0)
+
+    forward, relay, finish = share(buf, (sent, came, left, right, far), c, y, z, deep)
+    offer(0)
+    offer(1)
+    own_lse.wait()
+    for t in tell:
+        t.wait_recv()
+    tops = jnp.maximum(
+        jnp.maximum(levels[0], levels[1]), jnp.maximum(levels[2], levels[3])
+    )
+    weights = [jnp.exp2(levels[k] - tops) for k in range(4)]
+    scale = 1.0 / (weights[0] + weights[1] + weights[2] + weights[3])
+    for k in range(4):
+        alpha[k] = weights[k] * scale
+    for t in range(NZ + 3):
+        if t + 2 < NZ:
+            offer(t + 2)
+        if t < NZ:
+            add(t)
+        if 0 <= t - 1 < NZ:
+            complete(t - 1)
+        if t < NZ:
+            for p in added_to[t]:
+                p.start()
+        if 0 <= t - 1 < NZ:
+            scatter(t - 1)
+        if 0 <= t - 2 < NZ:
+            forward(t - 2)
+        if 0 <= t - 3 < NZ:
+            relay(t - 3)
+    for i in range(NZ):
+        dz = turn(i)
+        finish(i)
+        for p in offered[i] + added_to[i]:
+            p.wait_send()
+        if i == 0:
+            some = buf.at[0, pl.ds(0, 2 * NX - 1), 0, pl.ds(0, deep), :]
+            push(some, some, out_sem.at[dz], came.at[dz], c, y).wait_send()
+        else:
+            push(final.at[i], final.at[i], out_sem.at[dz], came.at[dz], c, y).wait_send()
+    for t in tell:
+        t.wait_send()
+
+
+def merge(parts, lse, deep):
+    def kernel(*refs):
+        merge_kernel(deep, *refs)
+
+    dma = pltpu.SemaphoreType.DMA
+    vmem = pl.BlockSpec(memory_space=pltpu.VMEM)
+    half = (2, NZ, 2, deep, BLOCK)
+    return pl.pallas_call(
+        kernel,
+        out_shape=jax.ShapeDtypeStruct((NX, NZ, 2, HD, HD), jnp.bfloat16),
+        in_specs=[vmem, vmem],
+        out_specs=vmem,
+        scratch_shapes=[
+            pltpu.VMEM((4, NX * NZ, 1, BLOCK), jnp.float32),
+            pltpu.VMEM((4, NX * NZ, 1, BLOCK), jnp.float32),
+            pltpu.VMEM(half, jnp.bfloat16),
+            pltpu.VMEM(half, jnp.bfloat16),
+            pltpu.VMEM(half, jnp.bfloat16),
+            pltpu.VMEM(half, jnp.bfloat16),
+            pltpu.VMEM((NZ, NX, deep, BLOCK), jnp.bfloat16),
+            dma((3,)), dma((4,)),
+            dma((2, NZ)), dma((2, NZ)), dma((2, NZ)), dma((2, NZ)), dma((2, NZ)), dma((2, NZ)),
+            dma((NZ,)), dma((NZ,)), dma((3, NZ)), dma((NZ,)), dma((NZ,)), dma((NZ,)),
+        ],
+        compiler_params=pltpu.CompilerParams(collective_id=2, has_side_effects=True),
+        name="merge",
+    )(parts, lse)
+
+
+def turn_kernel(src, dst):
+    for k in range(src.shape[0]):
+        dst[:, k * HD : (k + 1) * HD] = src[k].T
+
+
+def turned(heads):
+    count, _, rows = heads.shape
+    step = 8
+    return pl.pallas_call(
+        turn_kernel,
+        grid=(count // step,),
+        out_shape=jax.ShapeDtypeStruct((rows, count * HD), heads.dtype),
+        in_specs=[pl.BlockSpec((step, HD, rows), lambda i: (i, 0, 0))],
+        out_specs=pl.BlockSpec((rows, step * HD), lambda i: (0, i)),
+        name="turned",
+    )(heads)
+
+
 def shards(queries, keys, values, block_imgs, img_req, req_start):
     ctx = lax.axis_size("ctx")
     cache = lax.axis_size("cache")
@@ -296,17 +492,8 @@
     q = spread(queries, part).reshape(tokens, HD)
     out, lse = partial_attention(q, keys, values, block_imgs, img_req, req_start)
     deep = HD // cache
-    parts = lax.all_to_all(out.reshape(cache, deep, tokens), "cache", 0, 0)
-    levels = lax.all_gather(lse, "cache")
-    top = jnp.max(levels, axis=0)
-    weights = jnp.exp2(levels - top)
-    merged = jnp.sum(parts.astype(jnp.float32) * weights, axis=0) / jnp.sum(weights, axis=0)
-    merged = merged.astype(jnp.bfloat16)
-    mine = lax.all_to_all(
-        jnp.transpose(merged.reshape(deep, ctx, rows), (1, 0, 2)), "ctx", 0, 0
-    )
-    every = lax.all_gather(mine, "cache")
-    return jnp.transpose(every, (3, 1, 0, 2)).reshape(rows, ctx * HD)
+    heads = merge(out.reshape(NX, NZ, HD, BLOCK), lse, deep)
+    return turned(heads.reshape(ctx, HD, rows))
 
 
 def solution(mesh):

time: 167 us -> 126 us (0.75); the launches traced: 165 us -> 126 us
  Pallas kernels: 57.5 us -> 124 us
  blocking collectives: 49.9 us -> 0 us
  waiting for transfers between devices: 30.2 us -> 0 us
  between operations: 13.5 us -> 0.02 us
  local copies, waits for them, and re-layouts: 7.12 us -> 1.38 us
  starting transfers between devices: 5.29 us -> 0 us
    pallas_call x1 -> x3, Pallas kernels: 16.9 us -> 83.7 us  [the longest x1 60.5 us: merge(): pl.pallas_call(kernel, out_shape=jax.ShapeDtypeStruct((NX, NZ, 2, HD, HD)...]
    all_gather x1 -> x0, waiting for transfers between devices: 30.2 us -> none  [shards(): every = lax.all_gather(mine, 'cache')]
    all_gather x1 -> x0, blocking collectives: 26.8 us -> none  [shards(): levels = lax.all_gather(lse, 'cache')]
    all_to_all x1 -> x0, blocking collectives: 23.1 us -> none  [shards(): lax.all_to_all(jnp.transpose(merged.reshape(deep, ctx, rows), (1, 0, 2)),...]
    all_to_all x1 -> x0, starting transfers between devices: 5.29 us -> none  [shards(): parts = lax.all_to_all(out.reshape(cache, deep, tokens), 'cache', 0, 0)]
    reshape x1 -> x0, local copies, waits for them, and re-layouts: 2.89 us -> none  [shards(): return jnp.transpose(every, (3, 1, 0, 2)).reshape(rows, ctx * HD)]
    transpose x2 -> x0, local copies, waits for them, and re-layouts: 2.58 us -> none  [the longest x1 2.23 us: shards(): return jnp.transpose(every, (3, 1, 0, 2)).reshape(rows, ctx * HD)]
  transfers between devices with their start and end apart: 2 -> 0, of which waited for: 1 -> 0; matrix products, arithmetic and copies ran while one was open for 0% -> 0% of each run, Pallas kernels for 0% -> 0%
where the time goes in v3:
time: 126 us
  Pallas kernels  124 us (98%)
  local copies, waits for them, and re-layouts  1.38 us (1%)
    pallas_call x1, Pallas kernels, merge(): pl.pallas_call(kernel, out_shape=jax.ShapeDtypeStruct((NX, NZ, 2, HD, HD)...  60.5 us
    pallas_call x1, Pallas kernels, spread(): pl.pallas_call(kernel, out_shape=jax.ShapeDtypeStruct((NX, NZ, 2, 4 * par...  40.6 us
    pallas_call x1, Pallas kernels, partial_attention(): pl.pallas_call(kernel, out_shape=(jax.ShapeDtypeStruct((tokens // BLOCK,...  17.1 us
    pallas_call x1, Pallas kernels, turned(): pl.pallas_call(turn_kernel, grid=(count // step,), out_shape=jax.ShapeDty...  6.02 us

profile of v3, /device:TPU:16, one launch (start us, length us, event | category | flops | bytes accessed | tf_op | source)
XLA Modules:
  0.0 125.7 jit_solution(1163046005501351442)
XLA Ops:
  0.0 1.4 %copy.7.refs_0_ = s32[32,16]{1,0:T(8,128)} copy(s32[32,16]{0,1:T(8,128)} %param.9) | data formatting | bytes 4096 | tf_op args[3]
  1.4 40.6 %spread.1 = bf16[4,8,2,128,128]{4,3,2,1,0:T(8,128)(2,1)} custom-call(bf16[128,8192]{1,0:T(8,128)(2,1)} %refs_0_.2), custom_call_target="tpu_custom_call" | custom-call | tf_op jit(solution)/shard_map/spread/pallas_call | solution.py:276
  42.0 17.1 %partial.1 = (bf16[32,128,256]{2,1,0:T(8,128)(2,1)}, f32[32,1,256]{2,1,0:T(1,128)}) custom-call(s32[32,16]{1,0:T(8,128)} %copy.7.refs_0_, s32[192]{0:T(256)} %refs_1_.1, s32[32]{0:T(128)} %refs_2_.1, bf16[8192,128]{1,0:T(8,128)(2,1)} %bitcast.3, bf16[48,64,128]{2,1,0:T(8,128)(2,1)} %refs_4_.1, bf16[48,64,128]{2,1,0:T(8,128)(2,1)} %refs_5_.1), custom_call_target="tpu_custom_call" | custom-call | tf_op jit(solution)/shard_map/partial/pallas_call | solution.py:126
  59.1 60.5 %merge.1 = bf16[4,8,2,128,128]{4,3,2,1,0:T(8,128)(2,1)} custom-call(bf16[4,8,128,256]{3,2,1,0:T(8,128)(2,1)} %bitcast.5, f32[32,1,256]{2,1,0:T(1,128)} %get-tuple-element.8.refs_1_), custom_call_target="tpu_custom_call" | custom-call | tf_op jit(solution)/shard_map/merge/pallas_call | solution.py:446
  119.6 6.0 %turned.1 = bf16[128,8192]{1,0:T(8,128)(2,1)} custom-call(bf16[64,128,128]{2,1,0:T(8,128)(2,1)} %bitcast.4), custom_call_target="tpu_custom_call" | custom-call | tf_op jit(solution)/shard_map/turned/pallas_call | solution.py:476

commit v4 on v3

--- a/solution.py
+++ b/solution.py
@@ -17,7 +17,7 @@
     images = owners.shape[0]
     requests = starts.shape[0]
     tokens = q.shape[0]
-    slots = lists.shape[1] // 2
+    slots = lists.shape[0] // 2
     first = lax.axis_index("cache") * held
     wide = BLOCK + HD
 
@@ -26,7 +26,7 @@
         for s in range(slots):
             picked[u, s] = 0
         for s in range(slots):
-            image = lists[r, slots + s]
+            image = lists[slots + s, r]
             local = image - first
             owner = owners[jnp.minimum(image, images - 1)]
             here = (image < images) & (owner == r) & (local >= 0) & (local < held)
@@ -394,8 +394,8 @@
         lax.fori_loop(1 if i == 0 else 0, 2 * NX, send, 0)
 
     forward, relay, finish = share(buf, (sent, came, left, right, far), c, y, z, deep)
-    offer(0)
-    offer(1)
+    for i in range(4):
+        offer(i)
     own_lse.wait()
     for t in tell:
         t.wait_recv()
@@ -406,22 +406,23 @@
     scale = 1.0 / (weights[0] + weights[1] + weights[2] + weights[3])
     for k in range(4):
         alpha[k] = weights[k] * scale
-    for t in range(NZ + 3):
-        if t + 2 < NZ:
-            offer(t + 2)
+    lead, done, onward, last = 4, 2, 4, 5
+    for t in range(NZ + last):
+        if t + lead < NZ:
+            offer(t + lead)
         if t < NZ:
             add(t)
-        if 0 <= t - 1 < NZ:
-            complete(t - 1)
+        if 0 <= t - done < NZ:
+            complete(t - done)
         if t < NZ:
             for p in added_to[t]:
                 p.start()
-        if 0 <= t - 1 < NZ:
-            scatter(t - 1)
-        if 0 <= t - 2 < NZ:
-            forward(t - 2)
-        if 0 <= t - 3 < NZ:
-            relay(t - 3)
+        if 0 <= t - done < NZ:
+            scatter(t - done)
+        if 0 <= t - onward < NZ:
+            forward(t - onward)
+        if 0 <= t - last < NZ:
+            relay(t - last)
     for i in range(NZ):
         dz = turn(i)
         finish(i)
@@ -490,7 +491,7 @@
     part = rows // cache
     tokens = rows * ctx
     q = spread(queries, part).reshape(tokens, HD)
-    out, lse = partial_attention(q, keys, values, block_imgs, img_req, req_start)
+    out, lse = partial_attention(q, keys, values, block_imgs.T, img_req, req_start)
     deep = HD // cache
     heads = merge(out.reshape(NX, NZ, HD, BLOCK), lse, deep)
     return turned(heads.reshape(ctx, HD, rows))

time: 126 us -> 118 us (0.937); the launches traced: 126 us -> 116 us
  Pallas kernels: 124 us -> 116 us
  local copies, waits for them, and re-layouts: 1.38 us -> 0 us
    pallas_call x1, Pallas kernels: 60.5 us -> 51.7 us  [merge(): pl.pallas_call(kernel, out_shape=jax.ShapeDtypeStruct((NX, NZ, 2, HD, HD)...]
    unnamed x1 -> x0, local copies, waits for them, and re-layouts: 1.38 us -> none
where the time goes in v4:
time: 118 us; the launch traced here: 116 us
  Pallas kernels  116 us (98%)
    pallas_call x1, Pallas kernels, merge(): pl.pallas_call(kernel, out_shape=jax.ShapeDtypeStruct((NX, NZ, 2, HD, HD)...  51.7 us
    pallas_call x1, Pallas kernels, spread(): pl.pallas_call(kernel, out_shape=jax.ShapeDtypeStruct((NX, NZ, 2, 4 * par...  40.7 us
    pallas_call x1, Pallas kernels, partial_attention(): pl.pallas_call(kernel, out_shape=(jax.ShapeDtypeStruct((tokens // BLOCK,...  17.3 us
    pallas_call x1, Pallas kernels, turned(): pl.pallas_call(turn_kernel, grid=(count // step,), out_shape=jax.ShapeDty...  6.02 us

profile of v4, /device:TPU:16, one launch (start us, length us, event | category | flops | bytes accessed | tf_op | source)
XLA Modules:
  0.0 115.6 jit_solution(239109249448988731)
XLA Ops:
  0.0 40.7 %spread.1 = bf16[4,8,2,128,128]{4,3,2,1,0:T(8,128)(2,1)} custom-call(bf16[128,8192]{1,0:T(8,128)(2,1)} %refs_0_.1), custom_call_target="tpu_custom_call" | custom-call | tf_op jit(solution)/shard_map/spread/pallas_call | solution.py:276
  40.7 17.3 %partial.1 = (bf16[32,128,256]{2,1,0:T(8,128)(2,1)}, f32[32,1,256]{2,1,0:T(1,128)}) custom-call(s32[16,32]{1,0:T(8,128)} %bitcast.7, s32[192]{0:T(256)} %refs_1_.1, s32[32]{0:T(128)} %refs_2_.1, bf16[8192,128]{1,0:T(8,128)(2,1)} %bitcast.4, bf16[48,64,128]{2,1,0:T(8,128)(2,1)} %refs_4_.1, bf16[48,64,128]{2,1,0:T(8,128)(2,1)} %refs_5_.1), custom_call_target="tpu_custom_call" | custom-call | tf_op jit(solution)/shard_map/partial/pallas_call | solution.py:126
  58.0 51.7 %merge.1 = bf16[4,8,2,128,128]{4,3,2,1,0:T(8,128)(2,1)} custom-call(bf16[4,8,128,256]{3,2,1,0:T(8,128)(2,1)} %bitcast.6, f32[32,1,256]{2,1,0:T(1,128)} %get-tuple-element.8.refs_1_), custom_call_target="tpu_custom_call" | custom-call | tf_op jit(solution)/shard_map/merge/pallas_call | solution.py:447
  109.6 6.0 %turned.1 = bf16[128,8192]{1,0:T(8,128)(2,1)} custom-call(bf16[64,128,128]{2,1,0:T(8,128)(2,1)} %bitcast.5), custom_call_target="tpu_custom_call" | custom-call | tf_op jit(solution)/shard_map/turned/pallas_call | solution.py:477

commit v5 on v0

v5 whole, which is shorter than its diff:
```python
import jax
import jax.numpy as jnp
from jax import lax
from jax.experimental import pallas as pl
from jax.experimental.pallas import tpu as pltpu
from jax.sharding import PartitionSpec as P

HD = 128
BLOCK = 256
NX = 4
NZ = 8
FAR = 1e30
SCALE2 = HD ** (-0.5) * 1.4426950408889634
MESH = pl.DeviceIdType.MESH
RELAY, WORK, ADD, DONE, ONWARD, LAST = 1, 3, 5, 7, 9, 10


def push(src, dst, sent, landed, ctx, cache):
    return pltpu.make_async_remote_copy(
        src_ref=src,
        dst_ref=dst,
        send_sem=sent,
        recv_sem=landed,
        device_id=(ctx, cache),
        device_id_type=MESH,
    )


def turn(i):
    return 0 if i == 0 else ((i + 1) // 2 if i % 2 else NZ - i // 2)


def greet(c, y, offsets):
    barrier = pltpu.get_barrier_semaphore()

    def ring(s, carry):
        pl.semaphore_signal(
            barrier, inc=1, device_id=(lax.rem(c + s, 2 * NX * NZ), y), device_id_type=MESH
        )
        return carry

    lax.fori_loop(1, 2 * NX * NZ, ring, 0)
    for o in offsets:
        pl.semaphore_signal(
            barrier, inc=1, device_id=(c, lax.rem(y + o, 4)), device_id_type=MESH
        )
    pl.semaphore_wait(barrier, 2 * NX * NZ - 1 + len(offsets))


def share(buf, sems, c, y, column, part):
    sent, came, left, right, far = sems
    up = lax.rem(y + 1, 4)
    down = lax.rem(y + 3, 4)

    def piece(i, who):
        return buf.at[:, column(i), :, pl.ds(who * part, part), :]

    def forward(i):
        own = piece(i, y)
        going = push(own, own, sent.at[0, i], left.at[i], c, up)
        push(own, own, sent.at[0, i], came.at[i], c, up).wait_recv()
        going.start()
        push(own, own, sent.at[1, i], right.at[i], c, down).start()

    def relay(i):
        if i % 2 == 0:
            got = piece(i, down)
            push(got, got, sent.at[2, i], left.at[i], c, up).wait_recv()
            push(got, got, sent.at[2, i], far.at[i], c, up).start()
        else:
            got = piece(i, up)
            push(got, got, sent.at[2, i], right.at[i], c, down).wait_recv()
            push(got, got, sent.at[2, i], far.at[i], c, down).start()

    def ready(i):
        if i % 2 == 0:
            got = piece(i, up)
            push(got, got, sent.at[2, i], right.at[i], c, down).wait_recv()
        else:
            got = piece(i, down)
            push(got, got, sent.at[2, i], left.at[i], c, up).wait_recv()
        got = piece(i, lax.rem(y + 2, 4))
        push(got, got, sent.at[2, i], far.at[i], c, up).wait_recv()

    def drain(i):
        own = piece(i, y)
        for k in range(3):
            push(own, own, sent.at[k, i], far.at[i], c, up).wait_send()

    return forward, relay, ready, drain


def score(rows, keys):
    return lax.dot_general(
        keys, rows, (((1,), (1,)), ((), ())), preferred_element_type=jnp.float32
    )


def weigh_values(vals, probs):
    return lax.dot_general(
        vals, probs, (((0,), (0,)), ((), ())), preferred_element_type=jnp.float32
    )


def attend_block(r, first, q0, q1, lists, owners, starts, k, v):
    held, lat, _ = k.shape
    images = owners.shape[0]
    slots = lists.shape[0] // 2
    sides = []
    for side in range(2):
        ids, gaps = [], []
        for s in range(slots):
            image = lists[side * slots + s, r]
            local = image - first
            owner = owners[jnp.minimum(image, images - 1)]
            here = (
                (image < images) & (owner == r - 1 + side) & (local >= 0) & (local < held)
            )
            ids.append(jnp.where(here, local, 0))
            gaps.append(jnp.where(here, 0.0, FAR))
        sides.append((ids, gaps))
    (old_ids, old_gaps), (ids, gaps) = sides
    keys = jnp.concatenate([k[i] for i in ids], axis=0)
    old_keys = jnp.concatenate([k[i] for i in old_ids], axis=0)
    new_scores = score(jnp.concatenate([q0, q1], axis=0), keys)
    old_scores = score(q0, old_keys)
    position = r * BLOCK + lax.broadcasted_iota(jnp.int32, (1, HD), 1)
    before = position < starts[r]
    probs = []
    halves = []
    for half in range(2):
        tile = []
        levels = []
        top = jnp.full((1, HD), -FAR, jnp.float32)
        for s in range(slots):
            span = slice(s * lat, (s + 1) * lat)
            if half == 0:
                block = jnp.where(before, old_scores[span], new_scores[span, :HD])
                gap = jnp.where(before, old_gaps[s], gaps[s])
            else:
                block = new_scores[span, HD:]
                gap = jnp.full((1, HD), gaps[s], jnp.float32)
            tile.append(block)
            levels.append(gap)
            top = jnp.maximum(top, jnp.max(block, axis=0, keepdims=True) - gap)
        top = jnp.where(top < -0.5 * FAR, 0.0, top)
        total = jnp.zeros((1, HD), jnp.float32)
        weights = []
        for s in range(slots):
            p = jnp.exp2((tile[s] - (top + levels[s])) * SCALE2)
            total = total + jnp.sum(p, axis=0, keepdims=True)
            weights.append(p.astype(jnp.bfloat16))
        probs.append(jnp.concatenate(weights, axis=0))
        halves.append((top, total))
    vals = jnp.concatenate([v[i] for i in ids], axis=0)
    old_vals = jnp.concatenate([v[i] for i in old_ids], axis=0)
    summed = weigh_values(vals, jnp.concatenate(probs, axis=1))
    old_summed = weigh_values(old_vals, probs[0])
    results = []
    for half in range(2):
        top, total = halves[half]
        seen = total > 0
        safe = jnp.where(seen, total, 1.0)
        level = jnp.where(seen, top * SCALE2 + jnp.log2(safe), -FAR)
        numer = summed[:, half * HD : (half + 1) * HD]
        if half == 0:
            numer = jnp.where(before, old_summed, numer)
        results.append((level, (numer * (1.0 / safe)).astype(jnp.bfloat16)))
    return results


def whole_kernel(
    part, lists, owners, starts, q, k_hbm, v_hbm, buf,
    qbuf, k, v, own, levels, alpha, relayed, raw, added, adding, final,
    kv_sem, q_out, q_came, q_sent, q_left, q_right, q_far,
    l_sent, l_came, a_sent, a_came, r_sent, r_came, m_sent, m_came,
    o_out, o_came, o_sent, o_left, o_right, o_far,
):
    c = lax.axis_index("ctx")
    y = lax.axis_index("cache")
    x = c // (2 * NZ)
    z = lax.rem(c // 2, NZ)
    core = lax.rem(c, 2)
    up = lax.rem(y + 1, 4)
    down = lax.rem(y + 3, 4)
    across = lax.rem(y + 2, 4)
    first = y * k.shape[0]
    rows = pl.ds(y * part, part)
    loads = [
        pltpu.make_async_copy(k_hbm, k, kv_sem.at[0]),
        pltpu.make_async_copy(v_hbm, v, kv_sem.at[1]),
    ]
    for load in loads:
        load.start()
    greet(c, y, (1, 2, 3))

    def behind(i):
        return lax.rem(z + NZ - turn(i), NZ)

    def ahead(i):
        return lax.rem(z + turn(i), NZ)

    def everyone(one, i):
        def send(j, carry):
            to_x = lax.rem(x + j // 2, NX)
            to_core = lax.rem(core + lax.rem(j, 2), 2)
            one(to_x, to_core)
            return carry

        lax.fori_loop(1 if i == 0 else 0, 2 * NX, send, 0)

    q_home = qbuf.at[x, z, core, rows, :]

    def q_block(to):
        return q.at[rows, pl.ds(pl.multiple_of(to * HD, HD), HD)]

    for i in range(NZ):

        def q_send(to_x, to_core):
            to = to_x * (2 * NZ) + ahead(i) * 2 + to_core
            push(q_block(to), q_home, q_out.at[i], q_came.at[i], to, y).start()

        if i == 0:
            pltpu.make_async_copy(q_block(c), q_home, q_came.at[0]).start()
        everyone(q_send, i)
    q_forward, q_relay, q_ready, q_drain = share(
        qbuf, (q_sent, q_came, q_left, q_right, q_far), c, y, behind, part
    )

    def work(i):
        q_ready(i)
        if i == 0:
            for load in loads:
                load.wait()
        zs = behind(i)

        def one(n, carry):
            results = attend_block(
                n * NZ + zs, first, qbuf[n, zs, 0], qbuf[n, zs, 1], lists, owners, starts, k, v
            )
            for half in range(2):
                level, block = results[half]
                levels[y, i, n, :, half * HD : (half + 1) * HD] = level
                own[i, n, :, half * HD : (half + 1) * HD] = block
            return carry

        lax.fori_loop(0, NX, one, 0)

    def deep(who):
        return pl.ds(pl.multiple_of(who * part, part), part)

    low, high = pl.ds(0, 2), pl.ds(2, 2)
    tell = [
        [
            push(levels.at[y, i], levels.at[y, i], l_sent.at[o - 1, i], l_came.at[o - 1, i],
                 c, lax.rem(y + o, 4))
            for o in (1, 2, 3)
        ]
        for i in range(NZ)
    ]
    offers = [
        (
            push(own.at[i, low, deep(across), :], relayed.at[0, i],
                 a_sent.at[0, i], a_came.at[0, i], c, up),
            push(own.at[i, high, deep(across), :], relayed.at[1, i],
                 a_sent.at[1, i], a_came.at[1, i], c, down),
            push(own.at[i, high, deep(up), :], raw.at[0, i],
                 r_sent.at[0, i], r_came.at[0, i], c, up),
            push(own.at[i, low, deep(down), :], raw.at[1, i],
                 r_sent.at[1, i], r_came.at[1, i], c, down),
        )
        for i in range(NZ)
    ]
    adds = [
        (
            push(adding.at[0, i], added.at[0, i], m_sent.at[0, i], m_came.at[0, i], c, up),
            push(adding.at[1, i], added.at[1, i], m_sent.at[1, i], m_came.at[1, i], c, down),
        )
        for i in range(NZ)
    ]

    def offer(i):
        for p in tell[i] + list(offers[i]):
            p.start()

    def weigh(who, i, n, block):
        return block.astype(jnp.float32) * alpha[who, i, n]

    def add(i):
        for p in tell[i]:
            p.wait_recv()
        tops = jnp.maximum(
            jnp.maximum(levels[0, i], levels[1, i]), jnp.maximum(levels[2, i], levels[3, i])
        )
        weights = [jnp.exp2(levels[w, i] - tops) for w in range(4)]
        scale = 1.0 / (weights[0] + weights[1] + weights[2] + weights[3])
        for w in range(4):
            alpha[w, i] = weights[w] * scale
        offers[i][0].wait_recv()
        offers[i][1].wait_recv()
        for n in range(2):
            adding[0, i, n] = (
                weigh(down, i, n, relayed[0, i, n]) + weigh(y, i, n, own[i, n, deep(up), :])
            ).astype(jnp.bfloat16)
            adding[1, i, n] = (
                weigh(up, i, n + 2, relayed[1, i, n])
                + weigh(y, i, n + 2, own[i, n + 2, deep(down), :])
            ).astype(jnp.bfloat16)

    def complete(i):
        offers[i][2].wait_recv()
        offers[i][3].wait_recv()
        for p in adds[i]:
            p.wait_recv()
        for n in range(2):
            final[i, n] = (
                weigh(y, i, n, own[i, n, deep(y), :])
                + added[0, i, n].astype(jnp.float32)
                + weigh(up, i, n, raw[1, i, n])
            ).astype(jnp.bfloat16)
            final[i, n + 2] = (
                weigh(y, i, n + 2, own[i, n + 2, deep(y), :])
                + added[1, i, n].astype(jnp.float32)
                + weigh(down, i, n + 2, raw[0, i, n])
            ).astype(jnp.bfloat16)

    o_home = buf.at[x, z, core, rows, :]

    def o_block(i, to_x, to_core):
        return final.at[i, to_x, :, pl.ds(pl.multiple_of(to_core * HD, HD), HD)]

    def scatter(i):
        def o_send(to_x, to_core):
            to = to_x * (2 * NZ) + behind(i) * 2 + to_core
            push(o_block(i, to_x, to_core), o_home, o_out.at[i], o_came.at[i], to, y).start()

        if i == 0:
            pltpu.make_async_copy(o_block(0, x, core), o_home, o_came.at[0]).start()
        everyone(o_send, i)

    o_forward, o_relay, o_ready, o_drain = share(
        buf, (o_sent, o_came, o_left, o_right, o_far), c, y, ahead, part
    )

    def at(t, lag):
        return 0 <= t - lag < NZ

    for t in range(NZ + LAST):
        if at(t, 0):
            q_forward(t)
        if at(t, RELAY):
            q_relay(t - RELAY)
        if at(t, WORK):
            work(t - WORK)
        if at(t, ADD):
            add(t - ADD)
        if at(t, DONE):
            complete(t - DONE)
        if at(t, WORK):
            offer(t - WORK)
        if at(t, ADD):
            for p in adds[t - ADD]:
                p.start()
        if at(t, DONE):
            scatter(t - DONE)
        if at(t, ONWARD):
            o_forward(t - ONWARD)
        if at(t, LAST):
            o_relay(t - LAST)
    for i in range(NZ):
        o_ready(i)
        for p in tell[i] + list(offers[i]) + list(adds[i]):
            p.wait_send()
        for which, out, came in ((q_drain, q_out, q_came), (o_drain, o_out, o_came)):
            which(i)
            if i == 0:
                some = buf.at[0, pl.ds(0, 2 * NX - 1), 0, pl.ds(0, part), :]
            else:
                some = buf.at[0, :, 0, pl.ds(0, part), :]
            push(some, some, out.at[i], came.at[i], c, y).wait_send()


def whole(queries, keys, values, lists, img_req, req_start, part):
    def kernel(*refs):
        whole_kernel(part, *refs)

    dma = pltpu.SemaphoreType.DMA
    smem = pl.BlockSpec(memory_space=pltpu.SMEM)
    far = pl.BlockSpec(memory_space=pl.ANY)
    half = pltpu.VMEM((2, NZ, 2, part, BLOCK), jnp.bfloat16)
    heads = (NX, NZ, 2, HD, HD)
    level = pltpu.VMEM((4, NZ, NX, 1, BLOCK), jnp.float32)
    one, two, three = dma((NZ,)), dma((2, NZ)), dma((3, NZ))
    return pl.pallas_call(
        kernel,
        out_shape=jax.ShapeDtypeStruct(heads, jnp.bfloat16),
        in_specs=[smem, smem, smem, far, far, far],
        out_specs=pl.BlockSpec(memory_space=pltpu.VMEM),
        scratch_shapes=[
            pltpu.VMEM(heads, jnp.bfloat16),
            pltpu.VMEM(keys.shape, jnp.bfloat16),
            pltpu.VMEM(keys.shape, jnp.bfloat16),
            pltpu.VMEM((NZ, NX, HD, BLOCK), jnp.bfloat16),
            level, level, half, half, half, half,
            pltpu.VMEM((NZ, NX, part, BLOCK), jnp.bfloat16),
            dma((2,)), one, one, three, one, one, one,
            three, three, two, two, two, two, two, two,
            one, one, three, one, one, one,
        ],
        compiler_params=pltpu.CompilerParams(collective_id=1, has_side_effects=True),
        name="whole",
    )(lists, img_req, req_start, queries, keys, values)


def turn_kernel(src, dst):
    row = lax.broadcasted_iota(jnp.int32, (HD, HD), 0)
    column = lax.broadcasted_iota(jnp.int32, (HD, HD), 1)
    unit = (row == column).astype(jnp.bfloat16)
    count = src.shape[0]
    flat = src[...].reshape(count * HD, HD)
    dst[...] = lax.dot_general(
        unit, flat, (((1,), (1,)), ((), ())), preferred_element_type=jnp.float32
    ).astype(jnp.bfloat16)


def turned(heads):
    count, _, rows = heads.shape
    step = 16
    return pl.pallas_call(
        turn_kernel,
        grid=(count // step,),
        out_shape=jax.ShapeDtypeStruct((rows, count * HD), heads.dtype),
        in_specs=[pl.BlockSpec((step, HD, rows), lambda i: (i, 0, 0))],
        out_specs=pl.BlockSpec((rows, step * HD), lambda i: (0, i)),
        name="turned",
    )(heads)


def shards(queries, keys, values, block_imgs, img_req, req_start):
    ctx = lax.axis_size("ctx")
    rows = queries.shape[0]
    part = rows // lax.axis_size("cache")
    heads = whole(queries, keys, values, block_imgs.T, img_req, req_start, part)
    return turned(heads.reshape(ctx, HD, rows))


def solution(mesh):
    placed = (P("ctx", None), P("cache", None, "ctx"), P("cache", None, "ctx"), P(), P(), P())
    return jax.shard_map(
        shards, mesh=mesh, in_specs=placed, out_specs=P("ctx", None), check_vma=False
    )
```

time: 689 us -> 90.3 us (0.13)
  local copies, waits for them, and re-layouts: 187 us -> 0 us
  waiting for transfers between devices: 179 us -> 0 us
  other arithmetic: 145 us -> 0 us
  Pallas kernels: 0 us -> 90.1 us
  blocking collectives: 84.8 us -> 0 us
  matrix products: 39.1 us -> 0 us
  loops' own time: 22 us -> 0 us
  between operations: 13.5 us -> 0.01 us
  starting transfers between devices: 12.4 us -> 0 us
    all_gather x1 -> x0, waiting for transfers between devices: 129 us -> none  [merged(): gathered = jax.tree.map(lambda a: lax.all_gather(a, axis), part)]
    add x38 -> x0, other arithmetic: 106 us -> none  [the longest x3 104 us: combine(): numer_left * jnp.transpose(left_scale)[:, :, None]]
    pallas_call x0 -> x2, Pallas kernels: none -> 90.1 us  [the longest x1 85.8 us: whole(): pl.pallas_call(kernel, out_shape=jax.ShapeDtypeStruct(heads, jnp.bfloat16...]
    gather x64 -> x0, local copies, waits for them, and re-layouts: 81.9 us -> none  [the longest x16 40.6 us: attend(): key_cache[safe_local]]
    all_to_all x1 -> x0, blocking collectives: 61.3 us -> none  [shards(): lax.all_to_all(head_output, 'ctx', split_axis=0, concat_axis=1, tiled=True)]
    all_to_all x1 -> x0, waiting for transfers between devices: 50.2 us -> none  [shards(): lax.all_to_all(queries, 'ctx', split_axis=1, concat_axis=0, tiled=True)]
    dot_general x32 -> x0, matrix products: 39.1 us -> none  [the longest x16 26.2 us: attend(): jnp.einsum('gthd,gkhd->ghtk', query_blocks, key_rows, preferred_element_t...]
    dynamic_slice x36 -> x0, local copies, waits for them, and re-layouts: 36.3 us -> none  [the longest x16 14.7 us: one_step(): lax.dynamic_slice_in_dim(head_rows, step_index * group_size * block_len,...]
  transfers between devices with their start and end apart: 2 -> 0, of which waited for: 2 -> 0; matrix products, arithmetic and copies ran while one was open for 0% -> 0% of each run, Pallas kernels for 0% -> 0%
where the time goes in v5:
time: 90.3 us; the launch traced here: 90.1 us
  Pallas kernels  90.1 us (100%)
    pallas_call x1, Pallas kernels, whole(): pl.pallas_call(kernel, out_shape=jax.ShapeDtypeStruct(heads, jnp.bfloat16...  85.8 us
    pallas_call x1, Pallas kernels, turned(): pl.pallas_call(turn_kernel, grid=(count // step,), out_shape=jax.ShapeDty...  4.31 us

profile of v5, /device:TPU:16, one launch (start us, length us, event | category | flops | bytes accessed | tf_op | source)
XLA Modules:
  0.0 90.1 jit_solution(8808670680489172314)
XLA Ops:
  0.0 85.8 %whole.1 = bf16[4,8,2,128,128]{4,3,2,1,0:T(8,128)(2,1)} custom-call(s32[16,32]{1,0:T(8,128)} %bitcast.3, s32[192]{0:T(256)} %refs_1_.1, s32[32]{0:T(128)} %refs_2_.1, bf16[128,8192]{1,0:T(8,128)(2,1)} %refs_3_.1, bf16[48,64,128]{2,1,0:T(8,128)(2,1)} %refs_4_.1, bf16[48,64,128]{2,1,0:T(8,128)(2,1)} %refs_5_.1), custom_call_target="tpu_custom_call" | custom-call | tf_op jit(solution)/shard_map/whole/pallas_call | solution.py:394
  85.8 4.3 %turned.1 = bf16[128,8192]{1,0:T(8,128)(2,1)} custom-call(bf16[64,128,128]{2,1,0:T(8,128)(2,1)} %bitcast.2), custom_call_target="tpu_custom_call" | custom-call | tf_op jit(solution)/shard_map/turned/pallas_call | solution.py:429

commit v6 on v5

--- a/solution.py
+++ b/solution.py
@@ -12,7 +12,8 @@
 FAR = 1e30
 SCALE2 = HD ** (-0.5) * 1.4426950408889634
 MESH = pl.DeviceIdType.MESH
-RELAY, WORK, ADD, DONE, ONWARD, LAST = 1, 3, 5, 7, 9, 10
+RELAY, WORK, ADD, DONE, ONWARD, LAST, TURN = 3, 6, 9, 12, 15, 17, 19
+DIRECT = ()
 
 
 def push(src, dst, sent, landed, ctx, cache):
@@ -47,7 +48,7 @@
     pl.semaphore_wait(barrier, 2 * NX * NZ - 1 + len(offsets))
 
 
-def share(buf, sems, c, y, column, part):
+def share(buf, sems, c, y, column, part, direct=()):
     sent, came, left, right, far = sems
     up = lax.rem(y + 1, 4)
     down = lax.rem(y + 3, 4)
@@ -63,6 +64,8 @@
         push(own, own, sent.at[1, i], right.at[i], c, down).start()
 
     def relay(i):
+        if i in direct:
+            return
         if i % 2 == 0:
             got = piece(i, down)
             push(got, got, sent.at[2, i], left.at[i], c, up).wait_recv()
@@ -73,10 +76,10 @@
             push(got, got, sent.at[2, i], far.at[i], c, down).start()
 
     def ready(i):
-        if i % 2 == 0:
+        if i % 2 == 0 or i in direct:
             got = piece(i, up)
             push(got, got, sent.at[2, i], right.at[i], c, down).wait_recv()
-        else:
+        if i % 2 or i in direct:
             got = piece(i, down)
             push(got, got, sent.at[2, i], left.at[i], c, up).wait_recv()
         got = piece(i, lax.rem(y + 2, 4))
@@ -84,7 +87,7 @@
 
     def drain(i):
         own = piece(i, y)
-        for k in range(3):
+        for k in range(2 if i in direct else 3):
             push(own, own, sent.at[k, i], far.at[i], c, up).wait_send()
 
     return forward, relay, ready, drain
@@ -170,9 +173,9 @@
 
 
 def whole_kernel(
-    part, lists, owners, starts, q, k_hbm, v_hbm, buf,
-    qbuf, k, v, own, levels, alpha, relayed, raw, added, adding, final,
-    kv_sem, q_out, q_came, q_sent, q_left, q_right, q_far,
+    part, lists, owners, starts, q, k_hbm, v_hbm, result,
+    buf, qbuf, k, v, own, levels, alpha, relayed, raw, added, adding, final,
+    kv_sem, q_out, q_more, q_came, q_sent, q_left, q_right, q_far,
     l_sent, l_came, a_sent, a_came, r_sent, r_came, m_sent, m_came,
     o_out, o_came, o_sent, o_left, o_right, o_far,
 ):
@@ -209,22 +212,27 @@
 
         lax.fori_loop(1 if i == 0 else 0, 2 * NX, send, 0)
 
-    q_home = qbuf.at[x, z, core, rows, :]
-
-    def q_block(to):
-        return q.at[rows, pl.ds(pl.multiple_of(to * HD, HD), HD)]
-
-    for i in range(NZ):
+    def q_hand(i, who, out, came):
+        span = pl.ds(pl.multiple_of(who * part, part), part)
+        home = qbuf.at[x, z, core, span, :]
+
+        def block(to):
+            return q.at[span, pl.ds(pl.multiple_of(to * HD, HD), HD)]
 
         def q_send(to_x, to_core):
             to = to_x * (2 * NZ) + ahead(i) * 2 + to_core
-            push(q_block(to), q_home, q_out.at[i], q_came.at[i], to, y).start()
+            push(block(to), home, out.at[i], came.at[i], to, y).start()
 
         if i == 0:
-            pltpu.make_async_copy(q_block(c), q_home, q_came.at[0]).start()
+            pltpu.make_async_copy(block(c), home, came.at[0]).start()
         everyone(q_send, i)
+
+    for i in range(NZ):
+        q_hand(i, y, q_out, q_came)
+    for i in DIRECT:
+        q_hand(i, across, q_more, q_far)
     q_forward, q_relay, q_ready, q_drain = share(
-        qbuf, (q_sent, q_came, q_left, q_right, q_far), c, y, behind, part
+        qbuf, (q_sent, q_came, q_left, q_right, q_far), c, y, behind, part, DIRECT
     )
 
     def work(i):
@@ -342,10 +350,22 @@
         buf, (o_sent, o_came, o_left, o_right, o_far), c, y, ahead, part
     )
 
+    row = lax.broadcasted_iota(jnp.int32, (HD, HD), 0)
+    column = lax.broadcasted_iota(jnp.int32, (HD, HD), 1)
+    unit = (row == column).astype(jnp.bfloat16)
+
+    def turned(i):
+        o_ready(i)
+        zs = ahead(i)
+        for n in range(NX):
+            heads = buf[n, zs].reshape(2 * HD, HD)
+            to = pl.multiple_of((n * NZ + zs) * 2 * HD, 2 * HD)
+            result[:, pl.ds(to, 2 * HD)] = score(heads, unit).astype(jnp.bfloat16)
+
     def at(t, lag):
         return 0 <= t - lag < NZ
 
-    for t in range(NZ + LAST):
+    for t in range(NZ + TURN):
         if at(t, 0):
             q_forward(t)
         if at(t, RELAY):
@@ -367,8 +387,9 @@
             o_forward(t - ONWARD)
         if at(t, LAST):
             o_relay(t - LAST)
+        if at(t, TURN):
+            turned(t - TURN)
     for i in range(NZ):
-        o_ready(i)
         for p in tell[i] + list(offers[i]) + list(adds[i]):
             p.wait_send()
         for which, out, came in ((q_drain, q_out, q_came), (o_drain, o_out, o_came)):
@@ -378,6 +399,8 @@
             else:
                 some = buf.at[0, :, 0, pl.ds(0, part), :]
             push(some, some, out.at[i], came.at[i], c, y).wait_send()
+            if i in DIRECT and which is q_drain:
+                push(some, some, q_more.at[i], came.at[i], c, y).wait_send()
 
 
 def whole(queries, keys, values, lists, img_req, req_start, part):
@@ -393,17 +416,18 @@
     one, two, three = dma((NZ,)), dma((2, NZ)), dma((3, NZ))
     return pl.pallas_call(
         kernel,
-        out_shape=jax.ShapeDtypeStruct(heads, jnp.bfloat16),
+        out_shape=pltpu.VMEM((queries.shape[0], queries.shape[1]), jnp.bfloat16),
         in_specs=[smem, smem, smem, far, far, far],
         out_specs=pl.BlockSpec(memory_space=pltpu.VMEM),
         scratch_shapes=[
+            pltpu.VMEM(heads, jnp.bfloat16),
             pltpu.VMEM(heads, jnp.bfloat16),
             pltpu.VMEM(keys.shape, jnp.bfloat16),
             pltpu.VMEM(keys.shape, jnp.bfloat16),
             pltpu.VMEM((NZ, NX, HD, BLOCK), jnp.bfloat16),
             level, level, half, half, half, half,
             pltpu.VMEM((NZ, NX, part, BLOCK), jnp.bfloat16),
-            dma((2,)), one, one, three, one, one, one,
+            dma((2,)), one, one, one, three, one, one, one,
             three, three, two, two, two, two, two, two,
             one, one, three, one, one, one,
         ],
@@ -412,36 +436,9 @@
     )(lists, img_req, req_start, queries, keys, values)
 
 
-def turn_kernel(src, dst):
-    row = lax.broadcasted_iota(jnp.int32, (HD, HD), 0)
-    column = lax.broadcasted_iota(jnp.int32, (HD, HD), 1)
-    unit = (row == column).astype(jnp.bfloat16)
-    count = src.shape[0]
-    flat = src[...].reshape(count * HD, HD)
-    dst[...] = lax.dot_general(
-        unit, flat, (((1,), (1,)), ((), ())), preferred_element_type=jnp.float32
-    ).astype(jnp.bfloat16)
-
-
-def turned(heads):
-    count, _, rows = heads.shape
-    step = 16
-    return pl.pallas_call(
-        turn_kernel,
-        grid=(count // step,),
-        out_shape=jax.ShapeDtypeStruct((rows, count * HD), heads.dtype),
-        in_specs=[pl.BlockSpec((step, HD, rows), lambda i: (i, 0, 0))],
-        out_specs=pl.BlockSpec((rows, step * HD), lambda i: (0, i)),
-        name="turned",
-    )(heads)
-
-
 def shards(queries, keys, values, block_imgs, img_req, req_start):
-    ctx = lax.axis_size("ctx")
-    rows = queries.shape[0]
-    part = rows // lax.axis_size("cache")
-    heads = whole(queries, keys, values, block_imgs.T, img_req, req_start, part)
-    return turned(heads.reshape(ctx, HD, rows))
+    part = queries.shape[0] // lax.axis_size("cache")
+    return whole(queries, keys, values, block_imgs.T, img_req, req_start, part)
 
 
 def solution(mesh):

time: 90.3 us -> 78.9 us (0.87)
  Pallas kernels: 90.1 us -> 76.9 us
  local copies, waits for them, and re-layouts: 0 us -> 1.32 us
    pallas_call x2 -> x1, Pallas kernels: 90.1 us -> 76.9 us  [whole(): pl.pallas_call(kernel, out_shape=pltpu.VMEM((queries.shape[0], queries.sh...]
    unnamed x0 -> x1, local copies, waits for them, and re-layouts: none -> 1.32 us
where the time goes in v6:
time: 78.9 us; the launch traced here: 78.2 us
  Pallas kernels  76.9 us (97%)
  local copies, waits for them, and re-layouts  1.32 us (2%)
    pallas_call x1, Pallas kernels, whole(): pl.pallas_call(kernel, out_shape=pltpu.VMEM((queries.shape[0], queries.sh...  76.9 us

profile of v6, /device:TPU:16, one launch (start us, length us, event | category | flops | bytes accessed | tf_op | source)
XLA Modules:
  0.0 78.2 jit_solution(9544074390747277174)
XLA Ops:
  0.0 76.9 %whole.1 = bf16[128,8192]{1,0:T(8,128)(2,1)S(1)} custom-call(s32[16,32]{1,0:T(8,128)} %bitcast.1, s32[192]{0:T(256)} %refs_1_.1, s32[32]{0:T(128)} %refs_2_.1, bf16[128,8192]{1,0:T(8,128)(2,1)} %refs_3_.1, bf16[48,64,128]{2,1,0:T(8,128)(2,1)} %refs_4_.1, bf16[48,64,128]{2,1,0:T(8,128)(2,1)} %refs_5_.1), custom_call_target="tpu_custom_call" | custom-call | tf_op jit(solution)/shard_map/whole/pallas_call | solution.py:417
  76.9 1.3 %copy.8 = bf16[128,8192]{1,0:T(8,128)(2,1)} copy(bf16[128,8192]{1,0:T(8,128)(2,1)S(1)} %whole.1) | data formatting | bytes 4194304

commit v7 on v6

--- a/solution.py
+++ b/solution.py
@@ -12,8 +12,9 @@
 FAR = 1e30
 SCALE2 = HD ** (-0.5) * 1.4426950408889634
 MESH = pl.DeviceIdType.MESH
-RELAY, WORK, ADD, DONE, ONWARD, LAST, TURN = 3, 6, 9, 12, 15, 17, 19
-DIRECT = ()
+RELAY, WORK, ADD, DONE, ONWARD, LAST, TURN = 1, 2, 5, 8, 11, 13, 15
+DIRECT = (0, 1, 2, 3, 4, 5, 6, 7)
+PAIR = 4
 
 
 def push(src, dst, sent, landed, ctx, cache):
@@ -105,7 +106,7 @@
     )
 
 
-def attend_block(r, first, q0, q1, lists, owners, starts, k, v):
+def find_block(r, first, q0, q1, lists, owners, starts, k):
     held, lat, _ = k.shape
     images = owners.shape[0]
     slots = lists.shape[0] // 2
@@ -129,6 +130,12 @@
     old_scores = score(q0, old_keys)
     position = r * BLOCK + lax.broadcasted_iota(jnp.int32, (1, HD), 1)
     before = position < starts[r]
+    return before, sides, new_scores, old_scores
+
+
+def soften_block(state, slots, lat):
+    before, sides, new_scores, old_scores = state
+    (old_ids, old_gaps), (ids, gaps) = sides
     probs = []
     halves = []
     for half in range(2):
@@ -155,6 +162,13 @@
             weights.append(p.astype(jnp.bfloat16))
         probs.append(jnp.concatenate(weights, axis=0))
         halves.append((top, total))
+    return probs, halves
+
+
+def mix_block(state, soft, v):
+    before, sides, _, _ = state
+    (old_ids, _), (ids, _) = sides
+    probs, halves = soft
     vals = jnp.concatenate([v[i] for i in ids], axis=0)
     old_vals = jnp.concatenate([v[i] for i in old_ids], axis=0)
     summed = weigh_values(vals, jnp.concatenate(probs, axis=1))
@@ -229,8 +243,8 @@
 
     for i in range(NZ):
         q_hand(i, y, q_out, q_came)
-    for i in DIRECT:
-        q_hand(i, across, q_more, q_far)
+        if i in DIRECT:
+            q_hand(i, across, q_more, q_far)
     q_forward, q_relay, q_ready, q_drain = share(
         qbuf, (q_sent, q_came, q_left, q_right, q_far), c, y, behind, part, DIRECT
     )
@@ -242,17 +256,30 @@
                 load.wait()
         zs = behind(i)
 
-        def one(n, carry):
-            results = attend_block(
-                n * NZ + zs, first, qbuf[n, zs, 0], qbuf[n, zs, 1], lists, owners, starts, k, v
-            )
-            for half in range(2):
-                level, block = results[half]
-                levels[y, i, n, :, half * HD : (half + 1) * HD] = level
-                own[i, n, :, half * HD : (half + 1) * HD] = block
+        def some(g, carry):
+            blocks = [g * PAIR + m for m in range(PAIR)]
+            lat = k.shape[1]
+            slots = lists.shape[0] // 2
+            found = [
+                find_block(
+                    n * NZ + zs, first, qbuf[n, zs, 0], qbuf[n, zs, 1], lists, owners, starts, k
+                )
+                for n in blocks
+            ]
+            soft = [soften_block(found[0], slots, lat)]
+            results = []
+            for m in range(PAIR):
+                if m + 1 < PAIR:
+                    soft.append(soften_block(found[m + 1], slots, lat))
+                results.append(mix_block(found[m], soft[m], v))
+            for n, result in zip(blocks, results):
+                for half in range(2):
+                    level, block = result[half]
+                    levels[y, i, n, :, half * HD : (half + 1) * HD] = level
+                    own[i, n, :, half * HD : (half + 1) * HD] = block
             return carry
 
-        lax.fori_loop(0, NX, one, 0)
+        lax.fori_loop(0, NX // PAIR, some, 0)
 
     def deep(who):
         return pl.ds(pl.multiple_of(who * part, part), part)
@@ -362,6 +389,19 @@
             to = pl.multiple_of((n * NZ + zs) * 2 * HD, 2 * HD)
             result[:, pl.ds(to, 2 * HD)] = score(heads, unit).astype(jnp.bfloat16)
 
+    def settle(i):
+        for p in tell[i] + list(offers[i]) + list(adds[i]):
+            p.wait_send()
+        for which, out, came in ((q_drain, q_out, q_came), (o_drain, o_out, o_came)):
+            which(i)
+            if i == 0:
+                some = buf.at[0, pl.ds(0, 2 * NX - 1), 0, pl.ds(0, part), :]
+            else:
+                some = buf.at[0, :, 0, pl.ds(0, part), :]
+            push(some, some, out.at[i], came.at[i], c, y).wait_send()
+            if i in DIRECT and which is q_drain:
+                push(some, some, q_more.at[i], came.at[i], c, y).wait_send()
+
     def at(t, lag):
         return 0 <= t - lag < NZ
 
@@ -389,18 +429,7 @@
             o_relay(t - LAST)
         if at(t, TURN):
             turned(t - TURN)
-    for i in range(NZ):
-        for p in tell[i] + list(offers[i]) + list(adds[i]):
-            p.wait_send()
-        for which, out, came in ((q_drain, q_out, q_came), (o_drain, o_out, o_came)):
-            which(i)
-            if i == 0:
-                some = buf.at[0, pl.ds(0, 2 * NX - 1), 0, pl.ds(0, part), :]
-            else:
-                some = buf.at[0, :, 0, pl.ds(0, part), :]
-            push(some, some, out.at[i], came.at[i], c, y).wait_send()
-            if i in DIRECT and which is q_drain:
-                push(some, some, q_more.at[i], came.at[i], c, y).wait_send()
+            settle(t - TURN)
 
 
 def whole(queries, keys, values, lists, img_req, req_start, part):

time: 78.9 us -> 76.6 us (0.971)
  Pallas kernels: 76.9 us -> 75.1 us
    pallas_call x1, Pallas kernels: 76.9 us -> 75.1 us  [whole(): pl.pallas_call(kernel, out_shape=pltpu.VMEM((queries.shape[0], queries.sh...]
where the time goes in v7:
time: 76.6 us; the launch traced here: 76.5 us
  Pallas kernels  75.1 us (98%)
  local copies, waits for them, and re-layouts  1.32 us (2%)
    pallas_call x1, Pallas kernels, whole(): pl.pallas_call(kernel, out_shape=pltpu.VMEM((queries.shape[0], queries.sh...  75.1 us

profile of v7, /device:TPU:16, one launch (start us, length us, event | category | flops | bytes accessed | tf_op | source)
XLA Modules:
  0.0 76.5 jit_solution(16973616679533824032)
XLA Ops:
  0.0 75.1 %whole.1 = bf16[128,8192]{1,0:T(8,128)(2,1)S(1)} custom-call(s32[16,32]{1,0:T(8,128)} %bitcast.1, s32[192]{0:T(256)} %refs_1_.1, s32[32]{0:T(128)} %refs_2_.1, bf16[128,8192]{1,0:T(8,128)(2,1)} %refs_3_.1, bf16[48,64,128]{2,1,0:T(8,128)(2,1)} %refs_4_.1, bf16[48,64,128]{2,1,0:T(8,128)(2,1)} %refs_5_.1), custom_call_target="tpu_custom_call" | custom-call | tf_op jit(solution)/shard_map/whole/pallas_call | solution.py:446
  75.1 1.3 %copy.8 = bf16[128,8192]{1,0:T(8,128)(2,1)} copy(bf16[128,8192]{1,0:T(8,128)(2,1)S(1)} %whole.1) | data formatting | bytes 4194304

commit v8 on v7

--- a/solution.py
+++ b/solution.py
@@ -29,19 +29,24 @@
 
 
 def turn(i):
-    return 0 if i == 0 else ((i + 1) // 2 if i % 2 else NZ - i // 2)
+    return (1, 7, 2, 6, 3, 5, 4, 0)[i]
+
+
+def hops(shift):
+    dx, dz, _ = shift
+    return min(dx, NX - dx) + min(dz, NZ - dz)
 
 
 def greet(c, y, offsets):
     barrier = pltpu.get_barrier_semaphore()
-
-    def ring(s, carry):
+    xs = [lax.rem(c // (2 * NZ) + d, NX) * (2 * NZ) for d in range(NX)]
+    zs = [lax.rem(c // 2 + d, NZ) * 2 for d in range(NZ)]
+    cores = [lax.rem(c + d, 2) for d in range(2)]
+    shifts = [(dx, dz, dc) for dx in range(NX) for dz in range(NZ) for dc in range(2)]
+    for dx, dz, dc in sorted(shifts[1:], key=hops, reverse=True):
         pl.semaphore_signal(
-            barrier, inc=1, device_id=(lax.rem(c + s, 2 * NX * NZ), y), device_id_type=MESH
+            barrier, inc=1, device_id=(xs[dx] + zs[dz] + cores[dc], y), device_id_type=MESH
         )
-        return carry
-
-    lax.fori_loop(1, 2 * NX * NZ, ring, 0)
     for o in offsets:
         pl.semaphore_signal(
             barrier, inc=1, device_id=(c, lax.rem(y + o, 4)), device_id_type=MESH
@@ -217,14 +222,12 @@
     def ahead(i):
         return lax.rem(z + turn(i), NZ)
 
+    xs = [lax.rem(x + d, NX) for d in range(NX)]
+    cores = [lax.rem(core + d, 2) for d in range(2)]
+
     def everyone(one, i):
-        def send(j, carry):
-            to_x = lax.rem(x + j // 2, NX)
-            to_core = lax.rem(core + lax.rem(j, 2), 2)
-            one(to_x, to_core)
-            return carry
-
-        lax.fori_loop(1 if i == 0 else 0, 2 * NX, send, 0)
+        for j in range(1 if turn(i) == 0 else 0, 2 * NX):
+            one(xs[j // 2], cores[j % 2])
 
     def q_hand(i, who, out, came):
         span = pl.ds(pl.multiple_of(who * part, part), part)
@@ -237,8 +240,8 @@
             to = to_x * (2 * NZ) + ahead(i) * 2 + to_core
             push(block(to), home, out.at[i], came.at[i], to, y).start()
 
-        if i == 0:
-            pltpu.make_async_copy(block(c), home, came.at[0]).start()
+        if turn(i) == 0:
+            pltpu.make_async_copy(block(c), home, came.at[i]).start()
         everyone(q_send, i)
 
     for i in range(NZ):
@@ -369,8 +372,8 @@
             to = to_x * (2 * NZ) + behind(i) * 2 + to_core
             push(o_block(i, to_x, to_core), o_home, o_out.at[i], o_came.at[i], to, y).start()
 
-        if i == 0:
-            pltpu.make_async_copy(o_block(0, x, core), o_home, o_came.at[0]).start()
+        if turn(i) == 0:
+            pltpu.make_async_copy(o_block(i, x, core), o_home, o_came.at[i]).start()
         everyone(o_send, i)
 
     o_forward, o_relay, o_ready, o_drain = share(
@@ -394,7 +397,7 @@
             p.wait_send()
         for which, out, came in ((q_drain, q_out, q_came), (o_drain, o_out, o_came)):
             which(i)
-            if i == 0:
+            if turn(i) == 0:
                 some = buf.at[0, pl.ds(0, 2 * NX - 1), 0, pl.ds(0, part), :]
             else:
                 some = buf.at[0, :, 0, pl.ds(0, part), :]

time: 76.6 us -> 79.4 us (1.037)
  the two profiles are of different devices: /device:TPU:16 before, /device:TPU:56 now
where the time goes in v8:
time: 79.4 us; the launch traced here: 79.3 us
  Pallas kernels  78 us (98%)
  local copies, waits for them, and re-layouts  1.32 us (2%)
    pallas_call x1, Pallas kernels, whole(): pl.pallas_call(kernel, out_shape=pltpu.VMEM((queries.shape[0], queries.sh...  78 us

profile of v8, /device:TPU:56, one launch (start us, length us, event | category | flops | bytes accessed | tf_op | source)
XLA Modules:
  0.0 79.3 jit_solution(12337553656184314293)
XLA Ops:
  0.0 78.0 %whole.1 = bf16[128,8192]{1,0:T(8,128)(2,1)S(1)} custom-call(s32[16,32]{1,0:T(8,128)} %bitcast.1, s32[192]{0:T(256)} %refs_1_.1, s32[32]{0:T(128)} %refs_2_.1, bf16[128,8192]{1,0:T(8,128)(2,1)} %refs_3_.1, bf16[48,64,128]{2,1,0:T(8,128)(2,1)} %refs_4_.1, bf16[48,64,128]{2,1,0:T(8,128)(2,1)} %refs_5_.1), custom_call_target="tpu_custom_call" | custom-call | tf_op jit(solution)/shard_map/whole/pallas_call | solution.py:449
  78.0 1.3 %copy.8 = bf16[128,8192]{1,0:T(8,128)(2,1)} copy(bf16[128,8192]{1,0:T(8,128)(2,1)S(1)} %whole.1) | data formatting | bytes 4194304
